TPU v7x, 32 devices: a whole 2x2x4 slice. The times are simulated.
32 devices in a mesh: section: 8 (over z, x), tensor: 4 (over y, core).
Axes of the slice: x: 2, y: 2, z: 4, core: 2. Of those that a mesh axis runs over, the one named last changes fastest.
Arguments:
- noise: float32 [2, 4, 8, 32], P(None, None, 'tensor'), may hold values from -6 to 6
- target: float32 [2, 4, 8, 32], P(None, None, 'tensor'), may hold values from -6 to 6
- timesteps: int32 [8], replicated, may hold values from 1 to 160, as said below
- w_in: float32 [4, 320], replicated, may hold values from -3 to 3
- gn_gain: float32 [320], replicated, may hold values from 0.1 to 1.9
- w_time1: float32 [320, 1280], replicated, may hold values from -0.3125 to 0.3125
- w_time2: float32 [1280, 320], replicated, may hold values from -0.15625 to 0.15625
- w_conv: bfloat16 [9, 320, 320], replicated, may hold values from -0.109375 to 0.109375
- w_out: float32 [320, 4], replicated, may hold values from -0.3125 to 0.3125
Outputs:
- trajectory: float32 [8, 2, 4, 8, 32], P('section', None, None, 'tensor')
- grad_conv: float32 [9, 320, 320], P(None, None, 'tensor')
Inputs may be any that keep to these rules, and one draw needn't show every extreme that they name: `timesteps`: 8 distinct plan indices, strictly falling from one step to the next.
All inputs are finite; a program needn't handle non-finite values.
Results may differ from a plain program's by a relative error of at most 0.0008.
Values sent between devices are 32-bit elements; how exact they have to be, the bound alone decides.
A program may use at most 64 MiB of HBM per device.

v0:
```python
import math

import jax
import jax.numpy as jnp
from jax import lax
from jax.sharding import PartitionSpec as P

GROUPS = 32


precise = lax.Precision.HIGHEST


def extended(cells, sides, width):
    for axis, dim in sides:
        count = lax.axis_size(axis)
        ends = count - 1
        head = lax.slice_in_dim(cells, 0, width, axis=dim)
        tail = lax.slice_in_dim(cells, cells.shape[dim] - width, cells.shape[dim], axis=dim)
        cells = jnp.concatenate(
            [
                lax.ppermute(tail, axis, [(i, (i + 1) % count) for i in range(ends)]),
                cells,
                lax.ppermute(head, axis, [((i + 1) % count, i) for i in range(ends)]),
            ],
            axis=dim,
        )
    return cells


def passed_along(block, axis, distance):
    devices = range(lax.axis_size(axis))
    route = [(i - distance, i) for i in devices if i - distance in devices]
    return lax.ppermute(block, axis, route)


def alpha_table():
    step_grid = jnp.arange(1000, dtype=jnp.float32)
    lowest = jnp.sqrt(jnp.asarray(0.00085, jnp.float32))
    highest = jnp.sqrt(jnp.asarray(0.012, jnp.float32))
    betas = (lowest + step_grid * ((highest - lowest) / 999.0)) ** 2
    return jnp.cumprod(1.0 - betas)


def section_terms(timesteps, section_index, alphas, w_time1, w_time2, features):
    positions = jnp.arange(timesteps.shape[0], dtype=jnp.int32)
    current = jnp.sum(jnp.where(positions == section_index, timesteps, 0))
    following = jnp.sum(jnp.where(positions == section_index + 1, timesteps, 0))
    step_grid = jnp.arange(alphas.shape[0], dtype=jnp.int32)
    alpha_now = jnp.sum(jnp.where(step_grid == current, alphas, 0.0))
    alpha_next = jnp.where(
        section_index + 1 < timesteps.shape[0],
        jnp.sum(jnp.where(step_grid == following, alphas, 0.0)),
        1.0,
    )
    keep_coef = jnp.sqrt(alpha_next / alpha_now)
    noise_coef = jnp.sqrt(1.0 - alpha_next) - keep_coef * jnp.sqrt(1.0 - alpha_now)
    half_width = features // 2
    frequency = jnp.exp(-math.log(10000.0) * jnp.arange(half_width, dtype=jnp.float32) / half_width)
    angles = current.astype(jnp.float32) * frequency
    sinusoid = jnp.concatenate([jnp.cos(angles), jnp.sin(angles)])
    hidden = jax.nn.silu(jnp.dot(sinusoid, w_time1, precision=precise))
    return (keep_coef, noise_coef, jnp.dot(hidden, w_time2, precision=precise))


def group_partial(latent, w_in, groups):
    projected = jnp.einsum("crw,cd->rwd", latent, w_in, precision=precise)
    grouped = projected.reshape(-1, groups, projected.shape[2] // groups)
    return (jnp.sum(grouped, axis=(0, 2)), jnp.sum(grouped * grouped, axis=(0, 2)))


def local(noise, target, timesteps, w_in, gn_gain, w_time1, w_time2, w_conv, w_out):
    sections = lax.axis_size("section")
    section_index = lax.axis_index("section")
    tensor_size = lax.axis_size("tensor")
    tensor_index = lax.axis_index("tensor")
    micro_count, channels, row_count, breadth = noise.shape
    features = w_in.shape[1]
    height = row_count * tensor_size
    count_all = jnp.asarray(height * breadth * (features // GROUPS), jnp.float32)
    alphas = alpha_table()
    keep_coef, noise_coef, embed = section_terms(
        timesteps, section_index, alphas, w_time1, w_time2, features
    )
    wide_conv = w_conv.astype(jnp.float32)
    global_rows = tensor_index * row_count - 1 + jnp.arange(row_count + 2, dtype=jnp.int32)
    row_mask = ((global_rows >= 0) & (global_rows < height)).astype(jnp.float32)
    ticks = sections + micro_count - 1

    def exchange_rows(block):
        return extended(block, (("tensor", 1),), 1)

    def total_stats(pair):
        return lax.psum((pair[0], pair[1]), "tensor")

    def prepare(latent_pad, group_sum, squares):
        projected = jnp.einsum("crw,cd->rwd", latent_pad, w_in, precision=precise)
        group_avg = group_sum / count_all
        group_var = squares / count_all - group_avg * group_avg
        average = jnp.repeat(group_avg, features // GROUPS)
        variance = jnp.repeat(group_var, features // GROUPS)
        activated = (
            jax.nn.silu((projected - average) * lax.rsqrt(variance + 1e-05) * gn_gain)
            * row_mask[:, None, None]
        )
        activated = activated + lax.stop_gradient(
            activated.astype(jnp.bfloat16).astype(jnp.float32) - activated
        )
        return (projected, jnp.pad(activated, ((0, 0), (1, 1), (0, 0))))

    def finish(latent_pad, projected, convolved):
        hidden = projected[1:-1] + convolved + embed
        guess = jnp.einsum("rwd,dc->crw", hidden, w_out, precision=precise)
        return keep_coef * latent_pad[:, 1:-1] + noise_coef * guess

    def step_rows(latent_pad, group_sum, squares):
        projected, activated = prepare(latent_pad, group_sum, squares)
        narrow = activated.astype(jnp.bfloat16)
        convolved = jnp.zeros((row_count, breadth, features), jnp.float32)
        for offset in range(9):
            shift_row = offset // 3
            shift_col = offset % 3
            window = narrow[shift_row : shift_row + row_count, shift_col : shift_col + breadth]
            convolved = convolved + jnp.einsum(
                "rwc,cd->rwd", window, w_conv[offset], preferred_element_type=jnp.float32
            )
        return finish(latent_pad, projected, convolved)

    def forward_tick(tick, carry):
        outgoing, saved_pad, saved_sum, saved_square, path = carry
        arrived = passed_along(outgoing, "section", 1)
        micro_index = tick - section_index
        active = (micro_index >= 0) & (micro_index < micro_count)
        slot = jnp.clip(micro_index, 0, micro_count - 1)
        starting = lax.dynamic_index_in_dim(noise, slot, 0, keepdims=False)
        latent = jnp.where(section_index == 0, starting, arrived)
        latent_pad = exchange_rows(latent)
        group_sum, squares = total_stats(group_partial(latent, w_in, GROUPS))
        stepped = lax.cond(
            active,
            lambda: step_rows(latent_pad, group_sum, squares),
            lambda: jnp.zeros_like(latent),
        )

        def store(buffer, value):
            return jnp.where(
                active, lax.dynamic_update_index_in_dim(buffer, value, slot, 0), buffer
            )

        return (
            stepped,
            store(saved_pad, latent_pad),
            store(saved_sum, group_sum),
            store(saved_square, squares),
            store(path, stepped),
        )

    start_carry = (
        jnp.zeros_like(noise[0]),
        jnp.zeros((micro_count, channels, row_count + 2, breadth), jnp.float32),
        jnp.zeros((micro_count, GROUPS), jnp.float32),
        jnp.zeros((micro_count, GROUPS), jnp.float32),
        jnp.zeros_like(noise),
    )
    _, saved_pad, saved_sum, saved_square, path = lax.fori_loop(0, ticks, forward_tick, start_carry)

    def backward_tick(tick, carry):
        outgoing, grad_total = carry
        arrived = passed_along(outgoing, "section", -1)
        micro_index = tick - (sections - 1 - section_index)
        active = (micro_index >= 0) & (micro_index < micro_count)
        slot = jnp.clip(micro_index, 0, micro_count - 1)
        latent_pad = lax.dynamic_index_in_dim(saved_pad, slot, 0, keepdims=False)
        group_sum = lax.dynamic_index_in_dim(saved_sum, slot, 0, keepdims=False)
        squares = lax.dynamic_index_in_dim(saved_square, slot, 0, keepdims=False)
        finished = lax.dynamic_index_in_dim(
            path, slot, 0, keepdims=False
        ) - lax.dynamic_index_in_dim(target, slot, 0, keepdims=False)
        adjoint = jnp.where(section_index == sections - 1, finished, arrived)

        def pulled():
            (projected, activated), pre_pull = jax.vjp(prepare, latent_pad, group_sum, squares)
            blank = jnp.zeros((row_count, breadth, features), jnp.float32)
            _, post_pull = jax.vjp(finish, latent_pad, projected, blank)
            pad_first, proj_grad, conv_grad = post_pull(adjoint)
            act_grad = jnp.zeros_like(activated)
            weight_parts = []
            for offset in range(9):
                shift_row = offset // 3
                shift_col = offset % 3
                window = activated[
                    shift_row : shift_row + row_count, shift_col : shift_col + breadth
                ]
                back = jnp.einsum("rwd,cd->rwc", conv_grad, wide_conv[offset], precision=precise)
                act_grad = act_grad.at[
                    shift_row : shift_row + row_count, shift_col : shift_col + breadth
                ].add(back)
                weight_parts.append(jnp.einsum("rwc,rwd->cd", window, conv_grad, precision=precise))
            pad_second, sum_grad, square_grad = pre_pull((proj_grad, act_grad))
            return (
                pad_first + pad_second,
                sum_grad,
                square_grad,
                grad_total + jnp.stack(weight_parts),
            )

        def skipped():
            return (
                jnp.zeros_like(latent_pad),
                jnp.zeros_like(group_sum),
                jnp.zeros_like(squares),
                grad_total,
            )

        pad_grad, sum_grad, square_grad, grad_total = lax.cond(active, pulled, skipped)
        rims = jnp.concatenate([pad_grad[:, :1], pad_grad[:, -1:]], axis=1)
        moved = exchange_rows(rims)
        sum_total, square_total = total_stats((sum_grad, square_grad))
        _, stat_pull = jax.vjp(
            lambda own_rows: group_partial(own_rows, w_in, GROUPS), latent_pad[:, 1:-1]
        )
        own_grad = stat_pull((sum_total, square_total))[0]
        result = pad_grad[:, 1:-1] + own_grad
        result = result.at[:, 0].add(moved[:, 0]).at[:, -1].add(moved[:, 3])
        return (jnp.where(active, result, 0.0), grad_total)

    _, grad_total = lax.fori_loop(
        0, ticks, backward_tick, (jnp.zeros_like(noise[0]), jnp.zeros_like(wide_conv))
    )
    summed = lax.psum(grad_total, "section")
    share = lax.psum_scatter(summed, "tensor", scatter_dimension=2, tiled=True)
    return (path[None], share)


def solution(mesh):
    placed = (
        P(None, None, "tensor", None),
        P(None, None, "tensor", None),
        P(),
        P(),
        P(),
        P(),
        P(),
        P(),
        P(),
    )
    return jax.shard_map(
        local,
        mesh=mesh,
        in_specs=placed,
        out_specs=(P("section", None, None, "tensor", None), P(None, None, "tensor")),
        check_vma=False,
    )
```

profile of v0, /device:TPU:0, one launch (start us, length us, event | category | flops | bytes accessed | tf_op | source)
XLA Modules:
  0.0 928.1 jit_solution(1412074934663175862)
XLA Ops:
  15.9 4.0 convert_element_type.50
  22.0 222.7 %while.55 = (s32[]{:T(128)}, f32[4,2,32]{2,0,1:T(4,128)}, f32[2,4,4,32]{3,1,2,0:T(4,128)S(1)}, f32[2,32]{1,0:T(2,128)S(1)}, f32[2,32]{1,0:T(2,128)S(1)}, /*index...) while((s32[]{:T(128)}, f32[4,2,32]{2,0,1:T(4,128)}, ...), condition=%wide.region_15.16_spmd.clone, body=%wide.region_6.0_spmd.clone.sunk | while | flops 122699776 | bytes 4856627 | solution.py:165
  22.0 4.9 collective-permute-start
  33.5 6.9 all-reduce.10
  40.5 12.7 %conditional.6 = (f32[4,2,32]{2,0,1:T(4,128)}, f32[1,4,2,32]{3,1,2,0:T(4,128)S(1)}) conditional(s32[]{:T(128)} %convert_element_type.72, () %tuple.193, (f32[]{:T(128)}, f32[4,2,32]{2,0,1:T(4,128)S(1)}, f32[]{:T(128)}, f32[4,4,32]{2,0,1:T(4,128)S(1)}, f32[4,320]{1,0:T(4,128)S(1)}, /*index=5*/f32[32]{0:T(128)S(1)}, f32[32]{0:T(128)S(1)}, ...), branch_computations={%region_13.13_spmd, %region_14.14_spmd} | conditional | flops 121652128 | bytes 4781352 | solution.py:139
  61.2 6.9 all-reduce.10
  68.2 12.7 %conditional.6 = (f32[4,2,32]{2,0,1:T(4,128)}, f32[1,4,2,32]{3,1,2,0:T(4,128)S(1)}) conditional(s32[]{:T(128)} %convert_element_type.72, () %tuple.193, (f32[]{:T(128)}, f32[4,2,32]{2,0,1:T(4,128)S(1)}, f32[]{:T(128)}, f32[4,4,32]{2,0,1:T(4,128)S(1)}, f32[4,320]{1,0:T(4,128)S(1)}, /*index=5*/f32[32]{0:T(128)S(1)}, f32[32]{0:T(128)S(1)}, ...), branch_computations={%region_13.13_spmd, %region_14.14_spmd} | conditional | flops 121652128 | bytes 4781352 | solution.py:139
  80.9 4.2 collective-permute-start
  91.7 6.9 all-reduce.10
  99.4 16.2 %collective-permute-start = (f32[4,2,32]{2,0,1:T(4,128)}, f32[4,2,32]{2,0,1:T(4,128)S(1)}, u32[]{:S(2)}, u32[]{:S(2)}) collective-permute-start(f32[4,2,32]{2,0,1:T(4,128)} %get-tuple-element.1616), channel_id=1, source_target_pairs={{0,4},{4,8},{8,12},{12,16},{16,20},{20,24},{24,28},{1,5},{5,9},{9,... | collective-permute-start | bytes 3080 | tf_op jit(solution)/shard_map/while/body/eval_jaxpr/ppermute | solution.py:34
  122.3 6.9 all-reduce.10
  129.9 4.2 collective-permute-start
  140.8 6.9 all-reduce.10
  148.4 15.8 %collective-permute-start = (f32[4,2,32]{2,0,1:T(4,128)}, f32[4,2,32]{2,0,1:T(4,128)S(1)}, u32[]{:S(2)}, u32[]{:S(2)}) collective-permute-start(f32[4,2,32]{2,0,1:T(4,128)} %get-tuple-element.1616), channel_id=1, source_target_pairs={{0,4},{4,8},{8,12},{12,16},{16,20},{20,24},{24,28},{1,5},{5,9},{9,... | collective-permute-start | bytes 3080 | tf_op jit(solution)/shard_map/while/body/eval_jaxpr/ppermute | solution.py:34
  170.8 6.9 all-reduce.10
  178.5 5.1 collective-permute-start
  190.2 6.9 all-reduce.10
  197.9 13.1 %collective-permute-start = (f32[4,2,32]{2,0,1:T(4,128)}, f32[4,2,32]{2,0,1:T(4,128)S(1)}, u32[]{:S(2)}, u32[]{:S(2)}) collective-permute-start(f32[4,2,32]{2,0,1:T(4,128)} %get-tuple-element.1616), channel_id=1, source_target_pairs={{0,4},{4,8},{8,12},{12,16},{16,20},{20,24},{24,28},{1,5},{5,9},{9,... | collective-permute-start | bytes 3080 | tf_op jit(solution)/shard_map/while/body/eval_jaxpr/ppermute | solution.py:34
  217.6 6.9 all-reduce.10
  225.3 5.1 collective-permute-start
  237.0 6.9 all-reduce.10
  247.1 539.5 %while.56 = (s32[]{:T(128)}, f32[4,2,32]{2,0,1:T(4,128)S(1)}, f32[9,320,320]{2,1,0:T(8,128)}, s32[]{:T(128)}, f32[2,4,4,32]{3,1,2,0:T(4,128)S(1)}, /*index=5*/f3...) while((s32[]{:T(128)}, f32[4,2,32]{2,0,1:T(4,128)S(1)}, ...), condition=%wide.region_26.27_spmd.clone, body=%wide.region_16.26_spmd.clone.sunk | while | flops 1424694528 | bytes 27073080 | solution.py:227
  248.5 14.2 %collective-permute-done.3 = f32[4,2,32]{2,0,1:T(4,128)S(1)} collective-permute-done((f32[4,2,32]{2,0,1:T(4,128)S(1)}, f32[4,2,32]{2,0,1:T(4,128)S(1)}, u32[]{:S(2)}, u32[]{:S(2)}) %collective-permute-start.3) | collective-permute-done | bytes 1056 | tf_op jit(solution)/shard_map/while/body/eval_jaxpr/ppermute | solution.py:34
  265.3 8.6 all-reduce.11
  276.4 5.3 collective-permute-done.3
  284.3 8.8 all-reduce.11
  295.6 13.3 %collective-permute-done.3 = f32[4,2,32]{2,0,1:T(4,128)S(1)} collective-permute-done((f32[4,2,32]{2,0,1:T(4,128)S(1)}, f32[4,2,32]{2,0,1:T(4,128)S(1)}, u32[]{:S(2)}, u32[]{:S(2)}) %collective-permute-start.3) | collective-permute-done | bytes 1056 | tf_op jit(solution)/shard_map/while/body/eval_jaxpr/ppermute | solution.py:34
  311.5 8.8 all-reduce.11
  322.7 5.3 collective-permute-done.3
  330.7 8.8 all-reduce.11
  341.9 14.2 %collective-permute-done.3 = f32[4,2,32]{2,0,1:T(4,128)S(1)} collective-permute-done((f32[4,2,32]{2,0,1:T(4,128)S(1)}, f32[4,2,32]{2,0,1:T(4,128)S(1)}, u32[]{:S(2)}, u32[]{:S(2)}) %collective-permute-start.3) | collective-permute-done | bytes 1056 | tf_op jit(solution)/shard_map/while/body/eval_jaxpr/ppermute | solution.py:34
  358.7 8.7 all-reduce.11
  370.0 5.3 collective-permute-done.3
  377.9 8.7 all-reduce.11
  389.2 12.7 %collective-permute-done.3 = f32[4,2,32]{2,0,1:T(4,128)S(1)} collective-permute-done((f32[4,2,32]{2,0,1:T(4,128)S(1)}, f32[4,2,32]{2,0,1:T(4,128)S(1)}, u32[]{:S(2)}, u32[]{:S(2)}) %collective-permute-start.3) | collective-permute-done | bytes 1056 | tf_op jit(solution)/shard_map/while/body/eval_jaxpr/ppermute | solution.py:34
  404.5 8.8 all-reduce.11
  415.8 264.3 %collective-permute-done.3 = f32[4,2,32]{2,0,1:T(4,128)S(1)} collective-permute-done((f32[4,2,32]{2,0,1:T(4,128)S(1)}, f32[4,2,32]{2,0,1:T(4,128)S(1)}, u32[]{:S(2)}, u32[]{:S(2)}) %collective-permute-start.3) | collective-permute-done | bytes 1056 | tf_op jit(solution)/shard_map/while/body/eval_jaxpr/ppermute | solution.py:34
  680.1 37.6 %conditional.7 = (f32[4,4,32]{2,0,1:T(4,128)S(1)}, f32[32]{0:T(128)S(1)}, f32[32]{0:T(128)S(1)}, f32[9,320,320]{2,1,0:T(8,128)}) conditional(s32[]{:T(128)} %convert_element_type.74, f32[9,320,320]{2,1,0:T(8,128)} %get-tuple-element.1679, (f32[]{:T(128)}, pred[]{:T(512)}, f32[2,4,2,32]{3,1,2,0:T(4,128)S(1)}, s32[]{:T(128)}, ...), branch_computations={%region_17.17_spmd, %region_18.23_spmd} | conditional | flops 1422665984 | bytes 26852650 | solution.py:215
  689.2 3.4 fusion.58
  712.7 5.0 add.300
  720.3 8.7 all-reduce.11
  731.5 5.0 collective-permute-done.3
  736.6 37.6 %conditional.7 = (f32[4,4,32]{2,0,1:T(4,128)S(1)}, f32[32]{0:T(128)S(1)}, f32[32]{0:T(128)S(1)}, f32[9,320,320]{2,1,0:T(8,128)}) conditional(s32[]{:T(128)} %convert_element_type.74, f32[9,320,320]{2,1,0:T(8,128)} %get-tuple-element.1679, (f32[]{:T(128)}, pred[]{:T(512)}, f32[2,4,2,32]{3,1,2,0:T(4,128)S(1)}, s32[]{:T(128)}, ...), branch_computations={%region_17.17_spmd, %region_18.23_spmd} | conditional | flops 1422665984 | bytes 26852650 | solution.py:215
  769.2 5.0 add.300
  776.8 8.7 all-reduce.11
  786.7 6.0 copy.18
  792.7 43.5 %reduce-scatter.2.cloned.1.call-done = f32[9,320,80]{1,2,0:T(8,128)} async-done(((f32[9,320,320]{1,2,0:T(8,128)}), f32[9,320,80]{1,2,0:T(8,128)}) %reduce-scatter.2.cloned.1.call-update) | async-done | bytes 921616 | tf_op jit(solution)/shard_map/reduce_scatter | solution.py:231
  836.9 82.1 %all-reduce.14.cloned.1.call-done = f32[9,320,80]{1,2,0:T(8,128)} async-done(((f32[9,320,80]{1,2,0:T(8,128)}), f32[9,320,80]{1,2,0:T(8,128)}) %all-reduce.14.cloned.1.call-update) | async-done | bytes 921616 | tf_op jit(solution)/shard_map/psum | solution.py:230
  (557 shorter events, 214.8 us)
Async XLA Ops:
  7.2 829.1 %reduce-scatter.2.cloned.1.call-start = ((), (), s32[]{:S(2)}) async-start(), calls=%async_computation.1 | async-start | bytes 5529600 | tf_op jit(solution)/shard_map/reduce_scatter | solution.py:231
  28.7 11.8 %collective-permute-start.1 = (f32[4,1,32]{2,0,1:T(4,128)S(1)}, f32[4,1,32]{2,0,1:T(4,128)S(1)}, u32[]{:S(2)}, u32[]{:S(2)}) collective-permute-start(f32[4,1,32]{2,0,1:T(4,128)S(1)} %get-tuple-element.1547), channel_id=1, source_target_pairs={{1,0},{2,1},{3,2},{5,4},{6,5},{7,6},{9,8},{10,9},{11,10},{13,12},{... | collective-permute-start | bytes 1544 | tf_op jit(solution)/shard_map/while/body/eval_jaxpr/ppermute | solution.py:24
  30.0 10.5 %collective-permute-start.2 = (f32[4,1,32]{2,0,1:T(4,128)S(1)}, f32[4,1,32]{2,0,1:T(4,128)S(1)}, u32[]{:S(2)}, u32[]{:S(2)}) collective-permute-start(f32[4,1,32]{2,0,1:T(4,128)S(1)} %get-tuple-element.1548), channel_id=1, source_target_pairs={{0,1},{1,2},{2,3},{4,5},{5,6},{6,7},{8,9},{9,10},{10,11},{12,13},{... | collective-permute-start | bytes 1544 | tf_op jit(solution)/shard_map/while/body/eval_jaxpr/ppermute | solution.py:22
  56.4 11.8 %collective-permute-start.1 = (f32[4,1,32]{2,0,1:T(4,128)S(1)}, f32[4,1,32]{2,0,1:T(4,128)S(1)}, u32[]{:S(2)}, u32[]{:S(2)}) collective-permute-start(f32[4,1,32]{2,0,1:T(4,128)S(1)} %get-tuple-element.1547), channel_id=1, source_target_pairs={{1,0},{2,1},{3,2},{5,4},{6,5},{7,6},{9,8},{10,9},{11,10},{13,12},{... | collective-permute-start | bytes 1544 | tf_op jit(solution)/shard_map/while/body/eval_jaxpr/ppermute | solution.py:24
  57.7 10.5 %collective-permute-start.2 = (f32[4,1,32]{2,0,1:T(4,128)S(1)}, f32[4,1,32]{2,0,1:T(4,128)S(1)}, u32[]{:S(2)}, u32[]{:S(2)}) collective-permute-start(f32[4,1,32]{2,0,1:T(4,128)S(1)} %get-tuple-element.1548), channel_id=1, source_target_pairs={{0,1},{1,2},{2,3},{4,5},{5,6},{6,7},{8,9},{9,10},{10,11},{12,13},{... | collective-permute-start | bytes 1544 | tf_op jit(solution)/shard_map/while/body/eval_jaxpr/ppermute | solution.py:22
  86.9 11.8 %collective-permute-start.1 = (f32[4,1,32]{2,0,1:T(4,128)S(1)}, f32[4,1,32]{2,0,1:T(4,128)S(1)}, u32[]{:S(2)}, u32[]{:S(2)}) collective-permute-start(f32[4,1,32]{2,0,1:T(4,128)S(1)} %get-tuple-element.1547), channel_id=1, source_target_pairs={{1,0},{2,1},{3,2},{5,4},{6,5},{7,6},{9,8},{10,9},{11,10},{13,12},{... | collective-permute-start | bytes 1544 | tf_op jit(solution)/shard_map/while/body/eval_jaxpr/ppermute | solution.py:24
  88.2 10.5 %collective-permute-start.2 = (f32[4,1,32]{2,0,1:T(4,128)S(1)}, f32[4,1,32]{2,0,1:T(4,128)S(1)}, u32[]{:S(2)}, u32[]{:S(2)}) collective-permute-start(f32[4,1,32]{2,0,1:T(4,128)S(1)} %get-tuple-element.1548), channel_id=1, source_target_pairs={{0,1},{1,2},{2,3},{4,5},{5,6},{6,7},{8,9},{9,10},{10,11},{12,13},{... | collective-permute-start | bytes 1544 | tf_op jit(solution)/shard_map/while/body/eval_jaxpr/ppermute | solution.py:22
  99.4 17.8 %collective-permute-start = (f32[4,2,32]{2,0,1:T(4,128)}, f32[4,2,32]{2,0,1:T(4,128)S(1)}, u32[]{:S(2)}, u32[]{:S(2)}) collective-permute-start(f32[4,2,32]{2,0,1:T(4,128)} %get-tuple-element.1616), channel_id=1, source_target_pairs={{0,4},{4,8},{8,12},{12,16},{16,20},{20,24},{24,28},{1,5},{5,9},{9,... | collective-permute-start | bytes 3080 | tf_op jit(solution)/shard_map/while/body/eval_jaxpr/ppermute | solution.py:34
  117.5 11.8 %collective-permute-start.1 = (f32[4,1,32]{2,0,1:T(4,128)S(1)}, f32[4,1,32]{2,0,1:T(4,128)S(1)}, u32[]{:S(2)}, u32[]{:S(2)}) collective-permute-start(f32[4,1,32]{2,0,1:T(4,128)S(1)} %get-tuple-element.1547), channel_id=1, source_target_pairs={{1,0},{2,1},{3,2},{5,4},{6,5},{7,6},{9,8},{10,9},{11,10},{13,12},{... | collective-permute-start | bytes 1544 | tf_op jit(solution)/shard_map/while/body/eval_jaxpr/ppermute | solution.py:24
  118.8 10.5 %collective-permute-start.2 = (f32[4,1,32]{2,0,1:T(4,128)S(1)}, f32[4,1,32]{2,0,1:T(4,128)S(1)}, u32[]{:S(2)}, u32[]{:S(2)}) collective-permute-start(f32[4,1,32]{2,0,1:T(4,128)S(1)} %get-tuple-element.1548), channel_id=1, source_target_pairs={{0,1},{1,2},{2,3},{4,5},{5,6},{6,7},{8,9},{9,10},{10,11},{12,13},{... | collective-permute-start | bytes 1544 | tf_op jit(solution)/shard_map/while/body/eval_jaxpr/ppermute | solution.py:22
  136.0 11.8 %collective-permute-start.1 = (f32[4,1,32]{2,0,1:T(4,128)S(1)}, f32[4,1,32]{2,0,1:T(4,128)S(1)}, u32[]{:S(2)}, u32[]{:S(2)}) collective-permute-start(f32[4,1,32]{2,0,1:T(4,128)S(1)} %get-tuple-element.1547), channel_id=1, source_target_pairs={{1,0},{2,1},{3,2},{5,4},{6,5},{7,6},{9,8},{10,9},{11,10},{13,12},{... | collective-permute-start | bytes 1544 | tf_op jit(solution)/shard_map/while/body/eval_jaxpr/ppermute | solution.py:24
  137.3 10.5 %collective-permute-start.2 = (f32[4,1,32]{2,0,1:T(4,128)S(1)}, f32[4,1,32]{2,0,1:T(4,128)S(1)}, u32[]{:S(2)}, u32[]{:S(2)}) collective-permute-start(f32[4,1,32]{2,0,1:T(4,128)S(1)} %get-tuple-element.1548), channel_id=1, source_target_pairs={{0,1},{1,2},{2,3},{4,5},{5,6},{6,7},{8,9},{9,10},{10,11},{12,13},{... | collective-permute-start | bytes 1544 | tf_op jit(solution)/shard_map/while/body/eval_jaxpr/ppermute | solution.py:22
  148.4 17.3 %collective-permute-start = (f32[4,2,32]{2,0,1:T(4,128)}, f32[4,2,32]{2,0,1:T(4,128)S(1)}, u32[]{:S(2)}, u32[]{:S(2)}) collective-permute-start(f32[4,2,32]{2,0,1:T(4,128)} %get-tuple-element.1616), channel_id=1, source_target_pairs={{0,4},{4,8},{8,12},{12,16},{16,20},{20,24},{24,28},{1,5},{5,9},{9,... | collective-permute-start | bytes 3080 | tf_op jit(solution)/shard_map/while/body/eval_jaxpr/ppermute | solution.py:34
  166.1 11.8 %collective-permute-start.1 = (f32[4,1,32]{2,0,1:T(4,128)S(1)}, f32[4,1,32]{2,0,1:T(4,128)S(1)}, u32[]{:S(2)}, u32[]{:S(2)}) collective-permute-start(f32[4,1,32]{2,0,1:T(4,128)S(1)} %get-tuple-element.1547), channel_id=1, source_target_pairs={{1,0},{2,1},{3,2},{5,4},{6,5},{7,6},{9,8},{10,9},{11,10},{13,12},{... | collective-permute-start | bytes 1544 | tf_op jit(solution)/shard_map/while/body/eval_jaxpr/ppermute | solution.py:24
  167.4 10.5 %collective-permute-start.2 = (f32[4,1,32]{2,0,1:T(4,128)S(1)}, f32[4,1,32]{2,0,1:T(4,128)S(1)}, u32[]{:S(2)}, u32[]{:S(2)}) collective-permute-start(f32[4,1,32]{2,0,1:T(4,128)S(1)} %get-tuple-element.1548), channel_id=1, source_target_pairs={{0,1},{1,2},{2,3},{4,5},{5,6},{6,7},{8,9},{9,10},{10,11},{12,13},{... | collective-permute-start | bytes 1544 | tf_op jit(solution)/shard_map/while/body/eval_jaxpr/ppermute | solution.py:22
  185.5 11.8 %collective-permute-start.1 = (f32[4,1,32]{2,0,1:T(4,128)S(1)}, f32[4,1,32]{2,0,1:T(4,128)S(1)}, u32[]{:S(2)}, u32[]{:S(2)}) collective-permute-start(f32[4,1,32]{2,0,1:T(4,128)S(1)} %get-tuple-element.1547), channel_id=1, source_target_pairs={{1,0},{2,1},{3,2},{5,4},{6,5},{7,6},{9,8},{10,9},{11,10},{13,12},{... | collective-permute-start | bytes 1544 | tf_op jit(solution)/shard_map/while/body/eval_jaxpr/ppermute | solution.py:24
  186.8 10.5 %collective-permute-start.2 = (f32[4,1,32]{2,0,1:T(4,128)S(1)}, f32[4,1,32]{2,0,1:T(4,128)S(1)}, u32[]{:S(2)}, u32[]{:S(2)}) collective-permute-start(f32[4,1,32]{2,0,1:T(4,128)S(1)} %get-tuple-element.1548), channel_id=1, source_target_pairs={{0,1},{1,2},{2,3},{4,5},{5,6},{6,7},{8,9},{9,10},{10,11},{12,13},{... | collective-permute-start | bytes 1544 | tf_op jit(solution)/shard_map/while/body/eval_jaxpr/ppermute | solution.py:22
  197.9 14.6 %collective-permute-start = (f32[4,2,32]{2,0,1:T(4,128)}, f32[4,2,32]{2,0,1:T(4,128)S(1)}, u32[]{:S(2)}, u32[]{:S(2)}) collective-permute-start(f32[4,2,32]{2,0,1:T(4,128)} %get-tuple-element.1616), channel_id=1, source_target_pairs={{0,4},{4,8},{8,12},{12,16},{16,20},{20,24},{24,28},{1,5},{5,9},{9,... | collective-permute-start | bytes 3080 | tf_op jit(solution)/shard_map/while/body/eval_jaxpr/ppermute | solution.py:34
  212.8 11.8 %collective-permute-start.1 = (f32[4,1,32]{2,0,1:T(4,128)S(1)}, f32[4,1,32]{2,0,1:T(4,128)S(1)}, u32[]{:S(2)}, u32[]{:S(2)}) collective-permute-start(f32[4,1,32]{2,0,1:T(4,128)S(1)} %get-tuple-element.1547), channel_id=1, source_target_pairs={{1,0},{2,1},{3,2},{5,4},{6,5},{7,6},{9,8},{10,9},{11,10},{13,12},{... | collective-permute-start | bytes 1544 | tf_op jit(solution)/shard_map/while/body/eval_jaxpr/ppermute | solution.py:24
  214.1 10.5 %collective-permute-start.2 = (f32[4,1,32]{2,0,1:T(4,128)S(1)}, f32[4,1,32]{2,0,1:T(4,128)S(1)}, u32[]{:S(2)}, u32[]{:S(2)}) collective-permute-start(f32[4,1,32]{2,0,1:T(4,128)S(1)} %get-tuple-element.1548), channel_id=1, source_target_pairs={{0,1},{1,2},{2,3},{4,5},{5,6},{6,7},{8,9},{9,10},{10,11},{12,13},{... | collective-permute-start | bytes 1544 | tf_op jit(solution)/shard_map/while/body/eval_jaxpr/ppermute | solution.py:22
  232.3 11.8 %collective-permute-start.1 = (f32[4,1,32]{2,0,1:T(4,128)S(1)}, f32[4,1,32]{2,0,1:T(4,128)S(1)}, u32[]{:S(2)}, u32[]{:S(2)}) collective-permute-start(f32[4,1,32]{2,0,1:T(4,128)S(1)} %get-tuple-element.1547), channel_id=1, source_target_pairs={{1,0},{2,1},{3,2},{5,4},{6,5},{7,6},{9,8},{10,9},{11,10},{13,12},{... | collective-permute-start | bytes 1544 | tf_op jit(solution)/shard_map/while/body/eval_jaxpr/ppermute | solution.py:24
  233.6 10.5 %collective-permute-start.2 = (f32[4,1,32]{2,0,1:T(4,128)S(1)}, f32[4,1,32]{2,0,1:T(4,128)S(1)}, u32[]{:S(2)}, u32[]{:S(2)}) collective-permute-start(f32[4,1,32]{2,0,1:T(4,128)S(1)} %get-tuple-element.1548), channel_id=1, source_target_pairs={{0,1},{1,2},{2,3},{4,5},{5,6},{6,7},{8,9},{9,10},{10,11},{12,13},{... | collective-permute-start | bytes 1544 | tf_op jit(solution)/shard_map/while/body/eval_jaxpr/ppermute | solution.py:22
  247.1 15.5 %collective-permute-start.3 = (f32[4,2,32]{2,0,1:T(4,128)S(1)}, f32[4,2,32]{2,0,1:T(4,128)S(1)}, u32[]{:S(2)}, u32[]{:S(2)}) collective-permute-start(f32[4,2,32]{2,0,1:T(4,128)S(1)} %broadcast_select_fusion.8), channel_id=1, source_target_pairs={{4,0},{8,4},{12,8},{16,12},{20,16},{24,20},{28,24},{5,1},{9,5},{13... | collective-permute-start | bytes 3080 | tf_op jit(solution)/shard_map/while/body/eval_jaxpr/ppermute | solution.py:34
  262.7 12.2 %collective-permute-start.4 = (f32[4,1,32]{2,0,1:T(4,128)S(1)}, f32[4,1,32]{2,0,1:T(4,128)S(1)}, u32[]{:S(2)}, u32[]{:S(2)}) collective-permute-start(f32[4,1,32]{2,0,1:T(4,128)S(1)} %get-tuple-element.1579), channel_id=1, source_target_pairs={{0,1},{1,2},{2,3},{4,5},{5,6},{6,7},{8,9},{9,10},{10,11},{12,13},{... | collective-permute-start | bytes 1544 | tf_op jit(solution)/shard_map/while/body/eval_jaxpr/ppermute | solution.py:22
  264.0 10.9 %collective-permute-start.5 = (f32[4,1,32]{2,0,1:T(4,128)S(1)}, f32[4,1,32]{2,0,1:T(4,128)S(1)}, u32[]{:S(2)}, u32[]{:S(2)}) collective-permute-start(f32[4,1,32]{2,0,1:T(4,128)S(1)} %get-tuple-element.1580), channel_id=1, source_target_pairs={{1,0},{2,1},{3,2},{5,4},{6,5},{7,6},{9,8},{10,9},{11,10},{13,12},{... | collective-permute-start | bytes 1544 | tf_op jit(solution)/shard_map/while/body/eval_jaxpr/ppermute | solution.py:24
  275.0 6.7 collective-permute-start.3
  281.7 12.4 %collective-permute-start.4 = (f32[4,1,32]{2,0,1:T(4,128)S(1)}, f32[4,1,32]{2,0,1:T(4,128)S(1)}, u32[]{:S(2)}, u32[]{:S(2)}) collective-permute-start(f32[4,1,32]{2,0,1:T(4,128)S(1)} %get-tuple-element.1579), channel_id=1, source_target_pairs={{0,1},{1,2},{2,3},{4,5},{5,6},{6,7},{8,9},{9,10},{10,11},{12,13},{... | collective-permute-start | bytes 1544 | tf_op jit(solution)/shard_map/while/body/eval_jaxpr/ppermute | solution.py:22
  283.0 11.1 %collective-permute-start.5 = (f32[4,1,32]{2,0,1:T(4,128)S(1)}, f32[4,1,32]{2,0,1:T(4,128)S(1)}, u32[]{:S(2)}, u32[]{:S(2)}) collective-permute-start(f32[4,1,32]{2,0,1:T(4,128)S(1)} %get-tuple-element.1580), channel_id=1, source_target_pairs={{1,0},{2,1},{3,2},{5,4},{6,5},{7,6},{9,8},{10,9},{11,10},{13,12},{... | collective-permute-start | bytes 1544 | tf_op jit(solution)/shard_map/while/body/eval_jaxpr/ppermute | solution.py:24
  294.2 14.6 %collective-permute-start.3 = (f32[4,2,32]{2,0,1:T(4,128)S(1)}, f32[4,2,32]{2,0,1:T(4,128)S(1)}, u32[]{:S(2)}, u32[]{:S(2)}) collective-permute-start(f32[4,2,32]{2,0,1:T(4,128)S(1)} %broadcast_select_fusion.8), channel_id=1, source_target_pairs={{4,0},{8,4},{12,8},{16,12},{20,16},{24,20},{28,24},{5,1},{9,5},{13... | collective-permute-start | bytes 3080 | tf_op jit(solution)/shard_map/while/body/eval_jaxpr/ppermute | solution.py:34
  308.9 12.4 %collective-permute-start.4 = (f32[4,1,32]{2,0,1:T(4,128)S(1)}, f32[4,1,32]{2,0,1:T(4,128)S(1)}, u32[]{:S(2)}, u32[]{:S(2)}) collective-permute-start(f32[4,1,32]{2,0,1:T(4,128)S(1)} %get-tuple-element.1579), channel_id=1, source_target_pairs={{0,1},{1,2},{2,3},{4,5},{5,6},{6,7},{8,9},{9,10},{10,11},{12,13},{... | collective-permute-start | bytes 1544 | tf_op jit(solution)/shard_map/while/body/eval_jaxpr/ppermute | solution.py:22
  310.2 11.1 %collective-permute-start.5 = (f32[4,1,32]{2,0,1:T(4,128)S(1)}, f32[4,1,32]{2,0,1:T(4,128)S(1)}, u32[]{:S(2)}, u32[]{:S(2)}) collective-permute-start(f32[4,1,32]{2,0,1:T(4,128)S(1)} %get-tuple-element.1580), channel_id=1, source_target_pairs={{1,0},{2,1},{3,2},{5,4},{6,5},{7,6},{9,8},{10,9},{11,10},{13,12},{... | collective-permute-start | bytes 1544 | tf_op jit(solution)/shard_map/while/body/eval_jaxpr/ppermute | solution.py:24
  321.4 6.7 collective-permute-start.3
  328.1 12.4 %collective-permute-start.4 = (f32[4,1,32]{2,0,1:T(4,128)S(1)}, f32[4,1,32]{2,0,1:T(4,128)S(1)}, u32[]{:S(2)}, u32[]{:S(2)}) collective-permute-start(f32[4,1,32]{2,0,1:T(4,128)S(1)} %get-tuple-element.1579), channel_id=1, source_target_pairs={{0,1},{1,2},{2,3},{4,5},{5,6},{6,7},{8,9},{9,10},{10,11},{12,13},{... | collective-permute-start | bytes 1544 | tf_op jit(solution)/shard_map/while/body/eval_jaxpr/ppermute | solution.py:22
  329.4 11.1 %collective-permute-start.5 = (f32[4,1,32]{2,0,1:T(4,128)S(1)}, f32[4,1,32]{2,0,1:T(4,128)S(1)}, u32[]{:S(2)}, u32[]{:S(2)}) collective-permute-start(f32[4,1,32]{2,0,1:T(4,128)S(1)} %get-tuple-element.1580), channel_id=1, source_target_pairs={{1,0},{2,1},{3,2},{5,4},{6,5},{7,6},{9,8},{10,9},{11,10},{13,12},{... | collective-permute-start | bytes 1544 | tf_op jit(solution)/shard_map/while/body/eval_jaxpr/ppermute | solution.py:24
  340.6 15.5 %collective-permute-start.3 = (f32[4,2,32]{2,0,1:T(4,128)S(1)}, f32[4,2,32]{2,0,1:T(4,128)S(1)}, u32[]{:S(2)}, u32[]{:S(2)}) collective-permute-start(f32[4,2,32]{2,0,1:T(4,128)S(1)} %broadcast_select_fusion.8), channel_id=1, source_target_pairs={{4,0},{8,4},{12,8},{16,12},{20,16},{24,20},{28,24},{5,1},{9,5},{13... | collective-permute-start | bytes 3080 | tf_op jit(solution)/shard_map/while/body/eval_jaxpr/ppermute | solution.py:34
  356.2 12.4 %collective-permute-start.4 = (f32[4,1,32]{2,0,1:T(4,128)S(1)}, f32[4,1,32]{2,0,1:T(4,128)S(1)}, u32[]{:S(2)}, u32[]{:S(2)}) collective-permute-start(f32[4,1,32]{2,0,1:T(4,128)S(1)} %get-tuple-element.1579), channel_id=1, source_target_pairs={{0,1},{1,2},{2,3},{4,5},{5,6},{6,7},{8,9},{9,10},{10,11},{12,13},{... | collective-permute-start | bytes 1544 | tf_op jit(solution)/shard_map/while/body/eval_jaxpr/ppermute | solution.py:22
  357.4 11.1 %collective-permute-start.5 = (f32[4,1,32]{2,0,1:T(4,128)S(1)}, f32[4,1,32]{2,0,1:T(4,128)S(1)}, u32[]{:S(2)}, u32[]{:S(2)}) collective-permute-start(f32[4,1,32]{2,0,1:T(4,128)S(1)} %get-tuple-element.1580), channel_id=1, source_target_pairs={{1,0},{2,1},{3,2},{5,4},{6,5},{7,6},{9,8},{10,9},{11,10},{13,12},{... | collective-permute-start | bytes 1544 | tf_op jit(solution)/shard_map/while/body/eval_jaxpr/ppermute | solution.py:24
  375.3 12.4 %collective-permute-start.4 = (f32[4,1,32]{2,0,1:T(4,128)S(1)}, f32[4,1,32]{2,0,1:T(4,128)S(1)}, u32[]{:S(2)}, u32[]{:S(2)}) collective-permute-start(f32[4,1,32]{2,0,1:T(4,128)S(1)} %get-tuple-element.1579), channel_id=1, source_target_pairs={{0,1},{1,2},{2,3},{4,5},{5,6},{6,7},{8,9},{9,10},{10,11},{12,13},{... | collective-permute-start | bytes 1544 | tf_op jit(solution)/shard_map/while/body/eval_jaxpr/ppermute | solution.py:22
  376.6 11.1 %collective-permute-start.5 = (f32[4,1,32]{2,0,1:T(4,128)S(1)}, f32[4,1,32]{2,0,1:T(4,128)S(1)}, u32[]{:S(2)}, u32[]{:S(2)}) collective-permute-start(f32[4,1,32]{2,0,1:T(4,128)S(1)} %get-tuple-element.1580), channel_id=1, source_target_pairs={{1,0},{2,1},{3,2},{5,4},{6,5},{7,6},{9,8},{10,9},{11,10},{13,12},{... | collective-permute-start | bytes 1544 | tf_op jit(solution)/shard_map/while/body/eval_jaxpr/ppermute | solution.py:24
  387.9 14.0 %collective-permute-start.3 = (f32[4,2,32]{2,0,1:T(4,128)S(1)}, f32[4,2,32]{2,0,1:T(4,128)S(1)}, u32[]{:S(2)}, u32[]{:S(2)}) collective-permute-start(f32[4,2,32]{2,0,1:T(4,128)S(1)} %broadcast_select_fusion.8), channel_id=1, source_target_pairs={{4,0},{8,4},{12,8},{16,12},{20,16},{24,20},{28,24},{5,1},{9,5},{13... | collective-permute-start | bytes 3080 | tf_op jit(solution)/shard_map/while/body/eval_jaxpr/ppermute | solution.py:34
  401.9 12.4 %collective-permute-start.4 = (f32[4,1,32]{2,0,1:T(4,128)S(1)}, f32[4,1,32]{2,0,1:T(4,128)S(1)}, u32[]{:S(2)}, u32[]{:S(2)}) collective-permute-start(f32[4,1,32]{2,0,1:T(4,128)S(1)} %get-tuple-element.1579), channel_id=1, source_target_pairs={{0,1},{1,2},{2,3},{4,5},{5,6},{6,7},{8,9},{9,10},{10,11},{12,13},{... | collective-permute-start | bytes 1544 | tf_op jit(solution)/shard_map/while/body/eval_jaxpr/ppermute | solution.py:22
  403.2 11.1 %collective-permute-start.5 = (f32[4,1,32]{2,0,1:T(4,128)S(1)}, f32[4,1,32]{2,0,1:T(4,128)S(1)}, u32[]{:S(2)}, u32[]{:S(2)}) collective-permute-start(f32[4,1,32]{2,0,1:T(4,128)S(1)} %get-tuple-element.1580), channel_id=1, source_target_pairs={{1,0},{2,1},{3,2},{5,4},{6,5},{7,6},{9,8},{10,9},{11,10},{13,12},{... | collective-permute-start | bytes 1544 | tf_op jit(solution)/shard_map/while/body/eval_jaxpr/ppermute | solution.py:24
  414.4 265.7 %collective-permute-start.3 = (f32[4,2,32]{2,0,1:T(4,128)S(1)}, f32[4,2,32]{2,0,1:T(4,128)S(1)}, u32[]{:S(2)}, u32[]{:S(2)}) collective-permute-start(f32[4,2,32]{2,0,1:T(4,128)S(1)} %broadcast_select_fusion.8), channel_id=1, source_target_pairs={{4,0},{8,4},{12,8},{16,12},{20,16},{24,20},{28,24},{5,1},{9,5},{13... | collective-permute-start | bytes 3080 | tf_op jit(solution)/shard_map/while/body/eval_jaxpr/ppermute | solution.py:34
  717.7 12.4 %collective-permute-start.4 = (f32[4,1,32]{2,0,1:T(4,128)S(1)}, f32[4,1,32]{2,0,1:T(4,128)S(1)}, u32[]{:S(2)}, u32[]{:S(2)}) collective-permute-start(f32[4,1,32]{2,0,1:T(4,128)S(1)} %get-tuple-element.1579), channel_id=1, source_target_pairs={{0,1},{1,2},{2,3},{4,5},{5,6},{6,7},{8,9},{9,10},{10,11},{12,13},{... | collective-permute-start | bytes 1544 | tf_op jit(solution)/shard_map/while/body/eval_jaxpr/ppermute | solution.py:22
  719.0 11.1 %collective-permute-start.5 = (f32[4,1,32]{2,0,1:T(4,128)S(1)}, f32[4,1,32]{2,0,1:T(4,128)S(1)}, u32[]{:S(2)}, u32[]{:S(2)}) collective-permute-start(f32[4,1,32]{2,0,1:T(4,128)S(1)} %get-tuple-element.1580), channel_id=1, source_target_pairs={{1,0},{2,1},{3,2},{5,4},{6,5},{7,6},{9,8},{10,9},{11,10},{13,12},{... | collective-permute-start | bytes 1544 | tf_op jit(solution)/shard_map/while/body/eval_jaxpr/ppermute | solution.py:24
  774.2 12.4 %collective-permute-start.4 = (f32[4,1,32]{2,0,1:T(4,128)S(1)}, f32[4,1,32]{2,0,1:T(4,128)S(1)}, u32[]{:S(2)}, u32[]{:S(2)}) collective-permute-start(f32[4,1,32]{2,0,1:T(4,128)S(1)} %get-tuple-element.1579), channel_id=1, source_target_pairs={{0,1},{1,2},{2,3},{4,5},{5,6},{6,7},{8,9},{9,10},{10,11},{12,13},{... | collective-permute-start | bytes 1544 | tf_op jit(solution)/shard_map/while/body/eval_jaxpr/ppermute | solution.py:22
  775.5 11.1 %collective-permute-start.5 = (f32[4,1,32]{2,0,1:T(4,128)S(1)}, f32[4,1,32]{2,0,1:T(4,128)S(1)}, u32[]{:S(2)}, u32[]{:S(2)}) collective-permute-start(f32[4,1,32]{2,0,1:T(4,128)S(1)} %get-tuple-element.1580), channel_id=1, source_target_pairs={{1,0},{2,1},{3,2},{5,4},{6,5},{7,6},{9,8},{10,9},{11,10},{13,12},{... | collective-permute-start | bytes 1544 | tf_op jit(solution)/shard_map/while/body/eval_jaxpr/ppermute | solution.py:24
  792.7 126.3 %all-reduce.14.cloned.1.call-start = ((), (), s32[]{:S(2)}) async-start(), calls=%async_computation.2 | async-start | bytes 2211840 | tf_op jit(solution)/shard_map/psum | solution.py:230
  (14 other events, 94.0 us)
Sparse Core Ops, SparseCore 0:
  792.8 43.3 reduce-scatter.1
  839.8 79.1 all-reduce.13
where the time goes:
time: 932 us; the launch traced here: 928 us
  waiting for transfers between devices  479 us (51%)
  starting transfers between devices  144 us (15%)
  blocking collectives  141 us (15%)
  matrix products  83.2 us (9%)
  local copies, waits for them, and re-layouts  37.6 us (4%)
  other arithmetic  24.2 us (3%)
  between operations  16.9 us (2%)
    ppermute x18, waiting for transfers between devices, passed_along(): return lax.ppermute(block, axis, route)  353 us
    psum x18, blocking collectives, total_stats(): return lax.psum((pair[0], pair[1]), 'tensor')  141 us
    psum x1, waiting for transfers between devices, local(): summed = lax.psum(grad_total, 'section')  82.1 us
    ppermute x18, starting transfers between devices, passed_along(): return lax.ppermute(block, axis, route)  81.4 us
    reduce_scatter x1, waiting for transfers between devices, local(): share = lax.psum_scatter(summed, 'tensor', scatter_dimension=2, tiled=True)  43.5 us
    ppermute x18, starting transfers between devices, extended(): lax.ppermute(tail, axis, [(i, (i + 1) % count) for i in range(ends)])  38.9 us
    dot_general x18, matrix products, pulled(): jnp.einsum('rwd,cd->rwc', conv_grad, wide_conv[offset], precision=precise)  34.9 us
    ppermute x18, starting transfers between devices, extended(): lax.ppermute(head, axis, [((i + 1) % count, i) for i in range(ends)])  23.3 us
  transfers between devices with their start and end apart: 56, of which 20 were waited for; matrix products, arithmetic and copies ran while one was open for 2% of the time, Pallas kernels for 0%

commit v1 on v0

v1 whole, which is shorter than its diff:
```python
import functools
import math

import jax
import jax.numpy as jnp
import numpy as np
from jax import lax
from jax.experimental import pallas as pl
from jax.experimental.pallas import tpu as pltpu
from jax.sharding import PartitionSpec as P

GROUPS = 32
MESH = pl.DeviceIdType.MESH
HIGH = lax.Precision.HIGHEST
F32 = jnp.float32
BF16 = jnp.bfloat16
R = 8
LANES = 128


def alpha_table():
    step_grid = jnp.arange(1000, dtype=F32)
    lowest = jnp.sqrt(jnp.asarray(0.00085, F32))
    highest = jnp.sqrt(jnp.asarray(0.012, F32))
    betas = (lowest + step_grid * ((highest - lowest) / 999.0)) ** 2
    return jnp.cumprod(1.0 - betas)


def step_terms(timesteps, features):
    steps = timesteps.shape[0]
    table = alpha_table()
    grid = jnp.arange(table.shape[0], dtype=jnp.int32)
    now = jnp.sum(jnp.where(grid[None] == timesteps[:, None], table[None], 0.0), axis=1)
    after = jnp.concatenate([now[1:], jnp.ones((1,), F32)])
    keep = jnp.sqrt(after / now)
    noise = jnp.sqrt(1.0 - after) - keep * jnp.sqrt(1.0 - now)
    half = features // 2
    frequency = jnp.exp(-math.log(10000.0) * jnp.arange(half, dtype=F32) / half)
    angles = timesteps.astype(F32)[:, None] * frequency[None]
    return keep, noise, jnp.concatenate([jnp.cos(angles), jnp.sin(angles)], axis=1)


def parts3(x):
    high = x.astype(BF16).astype(F32)
    rest = x - high
    mid = rest.astype(BF16).astype(F32)
    low = (rest - mid).astype(BF16).astype(F32)
    return high, mid, low


def parts2(x):
    high = x.astype(BF16)
    return high, (x - high.astype(F32)).astype(BF16)


def iota(shape, axis):
    return lax.broadcasted_iota(jnp.int32, shape, axis)


def nn(a, b, precision=None):
    return lax.dot_general(a, b, (((1,), (0,)), ((), ())), precision=precision, preferred_element_type=F32)


def nt(a, b, precision=None):
    return lax.dot_general(a, b, (((1,), (1,)), ((), ())), precision=precision, preferred_element_type=F32)


def tn(a, b, precision=None):
    return lax.dot_general(a, b, (((0,), (0,)), ((), ())), precision=precision, preferred_element_type=F32)


def wide(column, lanes):
    return jnp.concatenate([column] * (lanes // LANES), axis=1) if lanes > LANES else column


def chain_kernel(dims, keep_ref, noise_ref, x_ref, sinus_ref, win_ref, gain_ref, wout_ref, w1_hbm, w2_hbm, wc_hbm,
                 path_ref, g_ref, w1, w2, wc, sems, act_s, z_s, scale_s, avg_s, rstd_s, wext, sm6, smt, v3, vt3, w2t, mask, ebs, gacc):
    height, width, features, steps, chans, taps_side = dims
    taps = taps_side * taps_side
    lanes = height * width
    count = float(lanes * (features // GROUPS))
    per_group = features // GROUPS
    blocks = 1 + chans
    qrows = blocks * R
    tcols = taps * R

    copies = [pltpu.make_async_copy(src, dst, sems.at[i]) for i, (src, dst) in enumerate(((wc_hbm, wc), (w1_hbm, w1), (w2_hbm, w2)))]
    for copy in copies:
        copy.start()

    lane = iota((R, lanes), 1)
    row, col = lane // width, lane % width
    offsets = []
    for tap in range(taps):
        dy, dx = tap // taps_side - taps_side // 2, tap % taps_side - taps_side // 2
        offsets.append(dy * width + dx)
        ok = (row + dy >= 0) & (row + dy < height) & (col + dx >= 0) & (col + dx < width)
        mask[tap * R:(tap + 1) * R] = ok.astype(F32)

    win = win_ref[...]
    wout = wout_ref[...]
    def picker(cols):
        return (iota((chans, cols), 1) % R == iota((chans, cols), 0)).astype(F32)
    win_t = tn(win, picker(6 * qrows), HIGH)
    wout_t = nn(wout, picker(3 * tcols), HIGH)
    gain_col = tn(gain_ref[...], jnp.ones((1, LANES), F32), HIGH)
    woutT = jnp.transpose(wout_t[:, :LANES])[:R]
    win8 = jnp.concatenate([win, jnp.zeros((R - chans, features), F32)], axis=0) if chans < R else win

    pa, pb, pc = parts3(jnp.concatenate([win_t[:, :6 * R], nn(woutT, win_t[:, :6 * R], HIGH)], axis=0))
    blk = iota(pa.shape, 1) // R
    wext[...] = jnp.where((blk == 2) | (blk == 4), pb, jnp.where(blk == 5, pc, pa)).astype(BF16)

    qlane = iota(win_t.shape, 1)
    qblk = (qlane % qrows) // R
    prod = win_t
    for c in range(chans):
        prod = jnp.where(qblk == c + 1, win_t * win_t[:, c:c + 1], prod)
    member = (iota((features, features), 0) // per_group == iota((features, features), 1) // per_group).astype(BF16)
    sa, sb, sc = parts3(prod)
    sums = (nn(member, sa.astype(BF16)) + nn(member, sb.astype(BF16)) + nn(member, sc.astype(BF16))) * (1.0 / count)
    sa, sb, sc = parts3(sums)
    rep = qlane // qrows
    chosen = jnp.where((rep == 2) | (rep == 4), sb, jnp.where(rep == 5, sc, sa))
    sm6[:features] = jnp.where(qblk == 0, chosen, 0.0).astype(BF16)
    sm6[features:] = jnp.where(qblk == 0, 0.0, chosen).astype(BF16)
    pad = 2 * LANES if qrows > LANES else LANES
    sumsT = jnp.transpose(sums[:, :pad])[:qrows]
    th, tm = parts2(sumsT)
    smt[:qrows] = th
    smt[qrows:] = tm
    wh, wm = parts2(jnp.concatenate([win8, jnp.zeros((R, features), F32)], axis=0))
    w2t[:2 * R] = wh
    w2t[2 * R:] = wm

    copies[0].wait()
    oa, ob, oc = parts3(wout_t)
    tblk = iota(wout_t.shape, 1) // R % taps
    v = jnp.zeros((features, 3 * tcols), F32)
    for tap in range(taps):
        weights = wc[tap]
        for part in (oa, ob, oc):
            v = v + nn(weights, jnp.where(tblk == tap, part, 0.0).astype(BF16))
    both = nn(win8, wout_t, HIGH)
    both = jnp.where(iota(both.shape, 1) // R % taps == taps // 2, both, 0.0)
    v_all = jnp.concatenate([v, both], axis=0)
    va, vb, _ = parts3(v_all)
    third = iota(v_all.shape, 1) // tcols
    v3[...] = jnp.where(third == 1, vb, va).astype(BF16)
    cols = -(-3 * tcols // LANES) * LANES
    v_pad = jnp.concatenate([v, jnp.zeros((features, cols - 3 * tcols), F32)], axis=1) if cols > 3 * tcols else v
    vT = jnp.transpose(v_pad)[:3 * tcols]
    va, vb, vc = parts3(vT)
    third = iota(vT.shape, 0) // tcols
    vt3[...] = jnp.where(third == 1, vb, jnp.where(third == 2, vc, va)).astype(BF16)

    copies[1].wait()
    copies[2].wait()
    hidden = nn(sinus_ref[...], w1[...], HIGH)
    hidden = hidden * (1.0 / (1.0 + jnp.exp(-hidden)))
    embed = nn(hidden, w2[...], HIGH)
    embed_out = nt(woutT, embed, HIGH)
    for s in range(steps):
        ebs[s] = jnp.broadcast_to(embed_out[:, s:s + 1], (R, LANES))

    start = x_ref[0]
    target = x_ref[1]
    for n in range(2, x_ref.shape[0], 2):
        start = start + x_ref[n]
        target = target + x_ref[n + 1]

    def forward(s, x):
        xa, xb, xc = parts3(x)
        x6 = jnp.concatenate([xa, xb, xa, xc, xb, xa], axis=0).astype(BF16)
        projected = nn(wext[...], x6)
        q = jnp.concatenate([x] + [x * x[c:c + 1] for c in range(chans)], axis=0)
        qs = jnp.broadcast_to(jnp.sum(q, axis=1, keepdims=True), (qrows, LANES))
        qa, qb, qc = parts3(qs)
        q6 = jnp.concatenate([qa, qb, qa, qc, qb, qa], axis=0).astype(BF16)
        stats = nn(sm6[...], q6)
        average = stats[:features]
        variance = stats[features:] - average * average
        rstd = lax.rsqrt(variance + 1e-05)
        scale = rstd * gain_col
        avg_s[s] = average
        rstd_s[s] = rstd
        scale_s[s] = scale
        z = (projected[:features] - wide(average, lanes)) * wide(scale, lanes)
        z_s[s] = z
        act = (z * (0.5 * jnp.tanh(0.5 * z) + 0.5)).astype(BF16)
        act_s[s] = act
        y = nn(vt3[...], act)
        y = y[:tcols] + (y[tcols:2 * tcols] + y[2 * tcols:])
        guess = projected[features:] + wide(ebs[s], lanes)
        for tap in range(taps):
            piece = y[tap * R:(tap + 1) * R]
            if offsets[tap] % lanes:
                piece = pltpu.roll(piece, (-offsets[tap]) % lanes, 1) * mask[tap * R:(tap + 1) * R]
            guess = guess + piece
        x = keep_ref[s] * x + noise_ref[s] * guess
        path_ref[s + 1] = x
        return x

    path_ref[0] = start
    last = lax.fori_loop(0, steps, forward, start)
    gacc[...] = jnp.zeros_like(gacc)

    def backward(i, adjoint):
        s = steps - 1 - i
        a = noise_ref[s] * adjoint
        shifted = []
        for tap in range(taps):
            piece = a
            if offsets[tap] % lanes:
                piece = pltpu.roll(a * mask[tap * R:(tap + 1) * R], offsets[tap] % lanes, 1)
            shifted.append(piece)
        shifted = jnp.concatenate(shifted, axis=0)
        high = shifted.astype(BF16).astype(F32)
        low = shifted - high
        a3 = jnp.concatenate([high, high, low], axis=0).astype(BF16)
        grads = nn(v3[...], a3)
        gacc[...] += nt(jnp.concatenate([high, low], axis=0).astype(BF16), act_s[s])
        z = z_s[s]
        sig = 0.5 * jnp.tanh(0.5 * z) + 0.5
        slope = sig + z * sig * (1.0 - sig)
        dz = grads[:features] * slope
        dzs = dz * wide(scale_s[s], lanes)
        rstd = rstd_s[s]
        e1 = jnp.broadcast_to(jnp.sum(dzs, axis=1, keepdims=True), (features, LANES))
        e2 = jnp.broadcast_to(jnp.sum(dz * z, axis=1, keepdims=True), (features, LANES)) * (rstd * rstd)
        pair = jnp.concatenate([e2 * avg_s[s] - e1, e2], axis=1)
        ph, pm = parts2(pair)
        k = nn(smt[...], ph)
        k = k[:qrows] + k[qrows:] + nn(smt[:qrows], pm)
        dh, dm = parts2(dzs)
        direct = nn(w2t[...], dh)
        direct = direct[:R] + direct[2 * R:3 * R] + nn(w2t[:2 * R], dm)[:R]
        result = keep_ref[s] * adjoint + grads[features:] + direct + wide(k[:R, :LANES], lanes)
        x = path_ref[s]
        for c in range(chans):
            result = result - wide(k[(c + 1) * R:(c + 2) * R, LANES:], lanes) * x[c:c + 1]
        return result

    lax.fori_loop(0, steps, backward, last - target)
    g_ref[...] = gacc[:tcols] + gacc[tcols:]


def run_chain(x, keep, noise_coef, sinus, w_in, gn_gain, w_time1, w_time2, w_conv, w_out, height, width):
    chans, features = w_in.shape
    steps = keep.shape[0]
    temb = w_time1.shape[1]
    taps = w_conv.shape[0]
    side = math.isqrt(taps)
    lanes = height * width
    qrows = (1 + chans) * R
    tcols = taps * R
    vmem = pl.BlockSpec(memory_space=pltpu.VMEM)
    smem = pl.BlockSpec(memory_space=pltpu.SMEM)
    hbm = pl.BlockSpec(memory_space=pl.ANY)
    return pl.pallas_call(
        functools.partial(chain_kernel, (height, width, features, steps, chans, side)),
        out_shape=(jax.ShapeDtypeStruct((steps + 1, R, lanes), F32), jax.ShapeDtypeStruct((tcols, features), F32)),
        in_specs=[smem, smem, vmem, vmem, vmem, vmem, vmem, hbm, hbm, hbm],
        out_specs=(vmem, vmem),
        scratch_shapes=[
            pltpu.VMEM((features, temb), F32),
            pltpu.VMEM((temb, features), F32),
            pltpu.VMEM((taps, features, features), BF16),
            pltpu.SemaphoreType.DMA((3,)),
            pltpu.VMEM((steps, features, lanes), BF16),
            pltpu.VMEM((steps, features, lanes), F32),
            pltpu.VMEM((steps, features, LANES), F32),
            pltpu.VMEM((steps, features, LANES), F32),
            pltpu.VMEM((steps, features, LANES), F32),
            pltpu.VMEM((features + R, 6 * R), BF16),
            pltpu.VMEM((2 * features, 6 * qrows), BF16),
            pltpu.VMEM((2 * qrows, features), BF16),
            pltpu.VMEM((features + R, 3 * tcols), BF16),
            pltpu.VMEM((3 * tcols, features), BF16),
            pltpu.VMEM((4 * R, features), BF16),
            pltpu.VMEM((tcols, lanes), F32),
            pltpu.VMEM((steps, R, LANES), F32),
            pltpu.VMEM((2 * tcols, features), F32),
        ],
        compiler_params=pltpu.CompilerParams(vmem_limit_bytes=60 * 1024 * 1024),
        name="chain",
    )(keep, noise_coef, x, sinus, w_in, gn_gain.reshape(1, features), w_out, w_time1, w_time2, w_conv)


def barrier_with(peers):
    barrier = pltpu.get_barrier_semaphore()
    for peer in peers:
        pl.semaphore_signal(barrier, inc=1, device_id={"tensor": peer}, device_id_type=MESH)
    pl.semaphore_wait(barrier, len(peers))


def gather_kernel(size, micro, mine_ref, slots_ref, send, recv, own):
    me = lax.axis_index("tensor")
    peers = [lax.rem(me + d, size) for d in range(1, size)]
    barrier_with(peers)
    copies = []
    for d, peer in enumerate(peers):
        copies.append(pltpu.make_async_remote_copy(
            src_ref=mine_ref.at[lax.rem(peer, micro)], dst_ref=slots_ref.at[d + 1],
            send_sem=send.at[d], recv_sem=recv.at[d], device_id={"tensor": peer}, device_id_type=MESH))
    for copy in copies:
        copy.start()
    local = pltpu.make_async_copy(mine_ref.at[lax.rem(me, micro)], slots_ref.at[0], own)
    local.start()
    local.wait()
    for copy in copies:
        copy.wait()


def gather(mine, size, micro):
    vmem = pl.BlockSpec(memory_space=pltpu.VMEM)
    return pl.pallas_call(
        functools.partial(gather_kernel, size, micro),
        out_shape=jax.ShapeDtypeStruct((size,) + mine.shape[1:], F32),
        in_specs=[vmem],
        out_specs=vmem,
        scratch_shapes=[pltpu.SemaphoreType.DMA((size - 1,)), pltpu.SemaphoreType.DMA((size - 1,)), pltpu.SemaphoreType.DMA],
        compiler_params=pltpu.CompilerParams(collective_id=0, has_side_effects=True),
        name="gather",
    )(mine)


def swap_kernel(micro, path_ref, g_ref, paths_ref, gs_ref, send, recv, own):
    section = lax.axis_index("section")
    me = lax.axis_index("tensor")
    mine = lax.rem(me, micro)
    peers = [me - mine + lax.rem(mine + d, micro) for d in range(1, micro)]
    barrier_with(peers)
    copies = []
    for d, peer in enumerate(peers):
        for k, (src, dst) in enumerate(((path_ref.at[section + 1], paths_ref.at[mine]), (g_ref, gs_ref.at[mine]))):
            copies.append(pltpu.make_async_remote_copy(
                src_ref=src, dst_ref=dst, send_sem=send.at[d, k], recv_sem=recv.at[d, k],
                device_id={"tensor": peer}, device_id_type=MESH))
    for copy in copies:
        copy.start()
    first = pltpu.make_async_copy(path_ref.at[section + 1], paths_ref.at[mine], own.at[0])
    second = pltpu.make_async_copy(g_ref, gs_ref.at[mine], own.at[1])
    first.start()
    second.start()
    first.wait()
    second.wait()
    for copy in copies:
        copy.wait()


def swap(path, g, micro):
    vmem = pl.BlockSpec(memory_space=pltpu.VMEM)
    return pl.pallas_call(
        functools.partial(swap_kernel, micro),
        out_shape=(jax.ShapeDtypeStruct((micro,) + path.shape[1:], F32), jax.ShapeDtypeStruct((micro,) + g.shape, F32)),
        in_specs=[vmem, vmem],
        out_specs=(vmem, vmem),
        scratch_shapes=[pltpu.SemaphoreType.DMA((micro - 1, 2)), pltpu.SemaphoreType.DMA((micro - 1, 2)), pltpu.SemaphoreType.DMA((2,))],
        compiler_params=pltpu.CompilerParams(collective_id=1, has_side_effects=True),
        name="swap",
    )(path, g)


def local(noise, target, timesteps, w_in, gn_gain, w_time1, w_time2, w_conv, w_out):
    size = lax.axis_size("tensor")
    me = lax.axis_index("tensor")
    micro, chans, rows, width = noise.shape
    features = w_in.shape[1]
    taps = w_conv.shape[0]
    height = rows * size
    span = rows * width
    lanes = height * width
    keep, noise_coef, sinus = step_terms(timesteps, features)

    flat = jnp.stack([noise.reshape(micro, chans, span), target.reshape(micro, chans, span)], axis=1)
    flat = jnp.pad(flat, ((0, 0), (0, 0), (0, R - chans), (0, 0)))
    here = jnp.arange(lanes, dtype=jnp.int32)[None, None, None] // span == me
    placed = jnp.where(here, jnp.tile(flat, (1, 1, 1, size)), 0.0)
    slots = gather(placed, size, micro)
    x = slots.reshape(2 * size, R, lanes)
    path, g = run_chain(x, keep, noise_coef, sinus, w_in, gn_gain, w_time1, w_time2, w_conv, w_out, height, width)
    paths, gs = swap(path, g, micro)
    out_path = lax.dynamic_slice(paths, (0, 0, me * span), (micro, chans, span)).reshape(1, micro, chans, rows, width)
    total = jnp.sum(gs, axis=0).reshape(taps, R, features)[:, :chans]
    share = features // size
    w_share = lax.dynamic_slice(w_out, (me * share, 0), (share, chans))
    grad = jnp.einsum("kcd,ec->kde", total, w_share, precision=HIGH)
    return out_path, grad


def solution(mesh):
    placed = (P(None, None, "tensor", None), P(None, None, "tensor", None)) + (P(),) * 7
    return jax.shard_map(
        local,
        mesh=mesh,
        in_specs=placed,
        out_specs=(P("section", None, None, "tensor", None), P(None, None, "tensor")),
        check_vma=False,
    )
```

time: 932 us -> 47.6 us (0.05)
  waiting for transfers between devices: 479 us -> 0 us
  starting transfers between devices: 144 us -> 0 us
  blocking collectives: 141 us -> 0 us
  matrix products: 83.2 us -> 2.12 us
  Pallas kernels: 0 us -> 31.8 us
  local copies, waits for them, and re-layouts: 37.6 us -> 7.63 us
  other arithmetic: 24.2 us -> 4.96 us
  between operations: 16.9 us -> 0.7 us
    ppermute x54 -> x0, waiting for transfers between devices: 353 us -> none  [the longest x18 353 us: passed_along(): return lax.ppermute(block, axis, route)]
    ppermute x54 -> x0, starting transfers between devices: 143 us -> none  [the longest x18 81.4 us: passed_along(): return lax.ppermute(block, axis, route)]
    psum x18 -> x0, blocking collectives: 141 us -> none  [total_stats(): return lax.psum((pair[0], pair[1]), 'tensor')]
    psum x1 -> x0, waiting for transfers between devices: 82.1 us -> none  [local(): summed = lax.psum(grad_total, 'section')]
    dot_general x93 -> x1, matrix products: 83.2 us -> 2.12 us  [local(): grad = jnp.einsum('kcd,ec->kde', total, w_share, precision=HIGH)]
    reduce_scatter x1 -> x0, waiting for transfers between devices: 43.5 us -> none  [local(): share = lax.psum_scatter(summed, 'tensor', scatter_dimension=2, tiled=True)]
    pallas_call x0 -> x3, Pallas kernels: none -> 31.8 us  [the longest x1 22.5 us: run_chain(): pl.pallas_call(functools.partial(chain_kernel, (height, width, features,...]
    add x2 -> x0, other arithmetic: 9.92 us -> none  [pulled(): grad_total + jnp.stack(weight_parts)]
  transfers between devices with their start and end apart: 56 -> 0, of which waited for: 20 -> 0; matrix products, arithmetic and copies ran while one was open for 2% -> 0% of each run, Pallas kernels for 0% -> 0%
where the time goes in v1:
time: 47.6 us; the launch traced here: 47.2 us
  Pallas kernels  31.8 us (67%)
  local copies, waits for them, and re-layouts  7.63 us (16%)
  other arithmetic  4.96 us (10%)
  matrix products  2.12 us (4%)
  between operations  0.7 us (1%)
    pallas_call x1, Pallas kernels, run_chain(): pl.pallas_call(functools.partial(chain_kernel, (height, width, features,...  22.5 us
    pallas_call x1, Pallas kernels, gather(): pl.pallas_call(functools.partial(gather_kernel, size, micro), out_shape=j...  6.31 us
    unnamed x7, local copies, waits for them, and re-layouts  3.66 us
    pallas_call x1, Pallas kernels, swap(): pl.pallas_call(functools.partial(swap_kernel, micro), out_shape=(jax.Shap...  3.01 us
    dot_general x1, matrix products, local(): grad = jnp.einsum('kcd,ec->kde', total, w_share, precision=HIGH)  2.12 us
    another operation x2, local copies, waits for them, and re-layouts, local(): jnp.stack([noise.reshape(micro, chans, span), target.reshape(micro, chans...  1.56 us
    reduce_sum x1, other arithmetic, local(): total = jnp.sum(gs, axis=0).reshape(taps, R, features)[:, :chans]  0.96 us

profile of v1, /device:TPU:0, one launch (start us, length us, event | category | flops | bytes accessed | tf_op | source)
XLA Modules:
  0.0 47.2 jit_solution(14171473799846714623)
XLA Ops:
  0.7 0.3 reduce-window.9
  0.9 0.1 slice.16
  1.0 0.1 slice_reduce_fusion
  1.2 0.1 multiply_bitcast_fusion
  1.2 0.8 %select_reduce_fusion = f32[8]{0:T(128)S(1)} fusion(f32[1000]{0:T(1024)S(1)} %bitcast.12, s32[8]{0:T(128)} %param.11), kind=kLoop, calls=%fused_computation.2 | loop fusion | flops 23992 | bytes 4064 | tf_op jit(solution)/shard_map/reduce_sum | solution.py:33
  2.1 0.1 slice.19
  2.1 0.7 %multiply_subtract_fusion.1 = (f32[8]{0:T(128)}, f32[8]{0:T(128)}) fusion(f32[8]{0:T(128)S(1)} %select_reduce_fusion, f32[1]{0:T(128)} %constant.38.clone.1, f32[7]{0:T(128)S(1)} %slice.19), kind=kLoop, calls=%fused_computation.24 | loop fusion | flops 48 | bytes 128 | tf_op jit(solution)/shard_map/sub | solution.py:36
  2.8 0.8 %stack_reshape.6 = f32[2,1,4,64]{3,2,0,1:T(4,128)S(1)} reshape(f32[2,4,2,32]{3,2,1,0:T(2,128)} %param.9) | data formatting | bytes 4096 | tf_op jit(solution)/shard_map/stack;reshape | solution.py:376
  3.6 0.8 %stack_reshape.7 = f32[2,1,4,64]{3,2,0,1:T(4,128)S(1)} reshape(f32[2,4,2,32]{3,2,1,0:T(2,128)} %param.10) | data formatting | bytes 4096 | tf_op jit(solution)/shard_map/stack;reshape | solution.py:376
  4.4 0.1 tile.10
  4.5 0.6 %broadcast_select_fusion.mine_ref = f32[2,2,8,256]{3,2,1,0:T(8,128)} fusion(f32[2,2,8,256]{3,2,1,0:T(8,128)S(1)} %tile.10, pred[256]{0:T(512)(128)(4,1)S(1)} %fusion.4), kind=kLoop, calls=%fused_computation.4 | loop fusion | flops 8192 | bytes 65792 | tf_op jit(solution)/shard_map/jit(_where)/select_n | solution.py:379
  5.2 6.3 %gather.1 = f32[4,2,8,256]{3,2,1,0:T(8,128)} custom-call(f32[2,2,8,256]{3,2,1,0:T(8,128)} %broadcast_select_fusion.mine_ref), custom_call_target="tpu_custom_call" | custom-call | tf_op jit(solution)/shard_map/gather/pallas_call | solution.py:317
  11.5 0.7 %convert_element_type.5 = f32[8]{0:T(128)S(1)} convert(s32[8]{0:T(128)} %param.11) | non-fusion elementwise | flops 8 | bytes 64 | tf_op jit(solution)/shard_map/convert_element_type | solution.py:39
  12.1 0.1 multiply_cosine_fusion
  12.3 0.7 %pad_maximum_fusion.sinus_ref = f32[8,320]{1,0:T(8,128)} fusion(f32[8,160]{1,0:T(8,128)S(1)} %get-tuple-element.13, f32[8,160]{1,0:T(8,128)S(1)} %get-tuple-element.12), kind=kLoop, calls=%fused_computation.5 | loop fusion | flops 2560 | bytes 20480 | tf_op jit(solution)/shard_map/concatenate | solution.py:40
  12.9 0.0 copy-start
  12.9 0.0 copy-start.1
  12.9 2.8 %copy.19.w2_hbm = f32[1280,320]{1,0:T(8,128)} copy(f32[1280,320]{0,1:T(8,128)} %param.15) | data formatting | bytes 3276800 | tf_op args[6]
  15.8 0.0 copy-done
  15.8 0.8 %copy.18.wout_ref = f32[320,4]{1,0:T(8,128)} copy(f32[320,4]{0,1:T(4,128)S(1)} %copy-done) | data formatting | bytes 10240 | tf_op args[8]
  16.6 0.0 copy-done.1
  16.6 0.6 %reshape.84.gain_ref = f32[1,320]{1,0:T(1,128)} reshape(f32[320]{0:T(512)S(1)} %copy-done.1) | data formatting | bytes 2560 | tf_op jit(solution)/shard_map/reshape | solution.py:287
  17.2 22.5 %chain.1 = (f32[9,8,256]{2,1,0:T(8,128)}, f32[72,320]{1,0:T(8,128)}) custom-call(f32[8]{0:T(128)} %get-tuple-element.11.keep_ref, f32[8]{0:T(128)} %get-tuple-element.10.noise_ref, f32[8,8,256]{2,1,0:T(8,128)} %bitcast.11, f32[8,320]{1,0:T(8,128)} %pad_maximum_fusion.sinus_ref, f32[4,320]{1,0:T(4,128)} %win_ref.1, f32[1,320]{1,0:T(1,128)} %reshape.84.gain_ref, ...), custom_call_target="tpu_custom_call" | custom-call | tf_op jit(solution)/shard_map/chain/pallas_call | solution.py:260
  39.6 3.0 %swap.1 = (f32[2,8,256]{2,1,0:T(8,128)}, f32[2,72,320]{2,1,0:T(8,128)}) custom-call(f32[9,8,256]{2,1,0:T(8,128)} %get-tuple-element.6.path_ref, f32[72,320]{1,0:T(8,128)} %get-tuple-element.7.g_ref), custom_call_target="tpu_custom_call" | custom-call | tf_op jit(solution)/shard_map/swap/pallas_call | solution.py:354
  42.7 1.0 %reduce_sum.19 = f32[72,320]{1,0:T(8,128)S(1)} reduce(f32[2,72,320]{2,1,0:T(8,128)} %get-tuple-element.9, f32[]{:T(128)} %constant.37.clone.1), dimensions={0}, to_apply=%region_3.4 | reduce | flops 23040 | bytes 276484 | tf_op jit(solution)/shard_map/reduce_sum | solution.py:385
  43.6 2.1 %fusion = f32[9,320,80]{1,2,0:T(8,128)} fusion(f32[9,8,320]{2,1,0:T(8,128)S(1)} %bitcast.10, f32[320,4]{0,1:T(4,128)S(1)} %copy-done, s32[]{:T(128)S(6)} %select_n.28), kind=kOutput, calls=%fused_computation | convolution fusion | flops 11059200 | bytes 978948 | tf_op jit(solution)/shard_map/kcd,ec->kde/dot_general | solution.py:388
  45.8 0.8 %constant_dynamic-slice_fusion = f32[2,4,64]{2,1,0:T(4,128)S(1)} fusion(f32[2,8,256]{2,1,0:T(8,128)} %get-tuple-element.8, s32[]{:T(128)S(6)} %select_n.27), kind=kLoop, calls=%fused_computation.23 | loop fusion | bytes 4100 | tf_op jit(solution)/shard_map/dynamic_slice | solution.py:384
  46.5 0.7 %reshape.85 = f32[1,2,4,2,32]{4,3,2,1,0:T(2,128)} reshape(f32[2,4,64]{2,1,0:T(4,128)S(1)} %constant_dynamic-slice_fusion) | data formatting | bytes 4096 | tf_op jit(solution)/shard_map/reshape | solution.py:384
  (9 shorter events, 0.1 us)
Async XLA Ops:
  12.9 2.8 %copy-start = (f32[320,4]{0,1:T(4,128)S(1)}, f32[320,4]{0,1:T(4,128)}, u32[]{:S(2)}) copy-start(f32[320,4]{0,1:T(4,128)} %param.17) | copy-start | bytes 15364
  12.9 3.7 %copy-start.1 = (f32[320]{0:T(512)S(1)}, f32[320]{0:T(512)}, u32[]{:S(2)}) copy-start(f32[320]{0:T(512)} %param.13) | copy-start | bytes 3844

commit v2 on v1

v2 whole, which is shorter than its diff:
```python
import functools
import math

import jax
import jax.numpy as jnp
from jax import lax
from jax.experimental import pallas as pl
from jax.experimental.pallas import tpu as pltpu
from jax.sharding import PartitionSpec as P

GROUPS = 32
MESH = pl.DeviceIdType.MESH
HIGH = lax.Precision.HIGHEST
F32 = jnp.float32
BF16 = jnp.bfloat16
R = 8
LANES = 128


def parts3(x):
    high = x.astype(BF16).astype(F32)
    rest = x - high
    mid = rest.astype(BF16).astype(F32)
    low = (rest - mid).astype(BF16).astype(F32)
    return high, mid, low


def parts2(x):
    high = x.astype(BF16)
    return high, (x - high.astype(F32)).astype(BF16)


def iota(shape, axis):
    return lax.broadcasted_iota(jnp.int32, shape, axis)


def nn(a, b, precision=None):
    return lax.dot_general(a, b, (((1,), (0,)), ((), ())), precision=precision, preferred_element_type=F32)


def nt(a, b, precision=None):
    return lax.dot_general(a, b, (((1,), (1,)), ((), ())), precision=precision, preferred_element_type=F32)


def tn(a, b, precision=None):
    return lax.dot_general(a, b, (((0,), (0,)), ((), ())), precision=precision, preferred_element_type=F32)


def wide(column, lanes):
    return jnp.concatenate([column] * (lanes // LANES), axis=1) if lanes > LANES else column


def dot3(a, b, dot):
    ah, am = parts2(a)
    bh, bm = parts2(b)
    return dot(ah, bh) + dot(am, bh) + dot(ah, bm)


def everywhere(value, combine):
    for axis in (1, 0):
        step = value.shape[axis] // 2
        while step:
            value = combine(value, pltpu.roll(value, step, axis))
            step //= 2
    return value


def step_coefficients(ts_ref, steps, keep_s, noise_s):
    index = iota((R, LANES), 0) * LANES + iota((R, LANES), 1)
    lowest = jnp.sqrt(jnp.full((R, LANES), 0.00085, F32))
    highest = jnp.sqrt(jnp.full((R, LANES), 0.012, F32))
    betas = (lowest + index.astype(F32) * ((highest - lowest) / 999.0)) ** 2
    factors = 1.0 - betas
    bars = [everywhere(jnp.where(index <= ts_ref[s], factors, 1.0), jnp.multiply) for s in range(steps)]
    bars.append(jnp.ones((R, LANES), F32))
    for s in range(steps):
        keep = jnp.sqrt(bars[s + 1] / bars[s])
        keep_s[s] = keep
        noise_s[s] = jnp.sqrt(1.0 - bars[s + 1]) - keep * jnp.sqrt(1.0 - bars[s])


def sinusoid(ts_ref, steps, features):
    half = features // 2
    shape = (steps, features)
    row, lane = iota(shape, 0), iota(shape, 1)
    times = jnp.zeros(shape, jnp.int32)
    for s in range(steps):
        times = jnp.where(row == s, ts_ref[s], times)
    place = jnp.where(lane < half, lane, lane - half).astype(F32)
    angles = times.astype(F32) * jnp.exp(-math.log(10000.0) * place / half)
    return jnp.where(lane < half, jnp.cos(angles), jnp.sin(angles))


def chain_kernel(dims, ts_ref, noise_ref, target_ref, win_ref, gain_ref, wout_ref, w1_hbm, w2_hbm, wc_hbm,
                 paths_ref, g_ref, w1, w2, wc, sems, mine, slots, send, recv, path, arrived, gsend, garrived, send2, recv2,
                 act_s, z_s, scale_s, avg_s, rstd_s, wext, sm6, smt, v3, vt3, w2t, mask, ebs, gacc, keep_s, noise_s):
    height, width, features, steps, chans, taps_side, size, micro = dims
    taps = taps_side * taps_side
    lanes = height * width
    rows = height // size
    span = rows * width
    per_group = features // GROUPS
    count = float(lanes * per_group)
    blocks = 1 + chans
    qrows = blocks * R
    tcols = taps * R
    section = lax.axis_index("section")
    me = lax.axis_index("tensor")
    own = lax.rem(me, micro)

    barrier = pltpu.get_barrier_semaphore()
    peers = [lax.rem(me + d, size) for d in range(1, size)]
    for peer in peers:
        pl.semaphore_signal(barrier, inc=1, device_id={"tensor": peer}, device_id_type=MESH)
    copies = [pltpu.make_async_copy(src, dst, sems.at[i]) for i, (src, dst) in enumerate(((wc_hbm, wc), (w1_hbm, w1), (w2_hbm, w2)))]
    for copy in copies:
        copy.start()
    mine[...] = jnp.zeros_like(mine)
    for m in range(micro):
        for r in range(rows):
            mine[m, :chans, r * width:(r + 1) * width] = noise_ref[m, :, r, :]
            mine[m, R:R + chans, r * width:(r + 1) * width] = target_ref[m, :, r, :]
    pl.semaphore_wait(barrier, size - 1)
    spread = [pltpu.make_async_remote_copy(
        src_ref=mine.at[lax.rem(peer, micro)], dst_ref=slots.at[d], send_sem=send.at[d], recv_sem=recv.at[d],
        device_id={"tensor": peer}, device_id_type=MESH) for d, peer in enumerate(peers)]
    for copy in spread:
        copy.start()

    step_coefficients(ts_ref, steps, keep_s, noise_s)

    lane = iota((R, lanes), 1)
    row, col = lane // width, lane % width
    offsets = []
    for tap in range(taps):
        dy, dx = tap // taps_side - taps_side // 2, tap % taps_side - taps_side // 2
        offsets.append(dy * width + dx)
        ok = (row + dy >= 0) & (row + dy < height) & (col + dx >= 0) & (col + dx < width)
        mask[tap * R:(tap + 1) * R] = ok.astype(F32)

    win, woutT = win_ref[...], wout_ref[...]
    if chans < R:
        fill = jnp.zeros((R - chans, features), F32)
        win, woutT = jnp.concatenate([win, fill], axis=0), jnp.concatenate([woutT, fill], axis=0)

    def tiled(weights, cols):
        high, mid, low = (part.astype(BF16) for part in parts3(weights))
        picker = (iota((R, cols), 1) % R == iota((R, cols), 0)).astype(BF16)
        return tn(high, picker) + tn(mid, picker) + tn(low, picker)

    win_t = tiled(win, 6 * qrows)
    wout_t = tiled(woutT, 3 * tcols)
    gain_row = gain_ref[...].reshape(1, features)
    gain_col = tn(gain_row, jnp.ones((1, LANES), F32), HIGH)

    pa, pb, pc = parts3(jnp.concatenate([win_t[:, :6 * R], dot3(woutT, win_t[:, :6 * R], nn)], axis=0))
    blk = iota(pa.shape, 1) // R
    wext[...] = jnp.where((blk == 2) | (blk == 4), pb, jnp.where(blk == 5, pc, pa)).astype(BF16)

    qlane = iota(win_t.shape, 1)
    qblk = (qlane % qrows) // R
    factor = jnp.ones_like(win_t)
    for c in range(chans):
        factor = jnp.where(qblk == c + 1, win_t[:, c:c + 1], factor)
    member = (iota((features, features), 0) // per_group == iota((features, features), 1) // per_group).astype(BF16)
    sa, sb = parts2(win_t * factor)
    sums = (nn(member, sa) + nn(member, sb)) * (1.0 / count)
    sa, sb, sc = parts3(sums)
    rep = qlane // qrows
    chosen = jnp.where((rep == 2) | (rep == 4), sb, jnp.where(rep == 5, sc, sa))
    sm6[:features] = jnp.where(qblk == 0, chosen, 0.0).astype(BF16)
    sm6[features:] = jnp.where(qblk == 0, 0.0, chosen).astype(BF16)
    pad = -(-qrows // LANES) * LANES
    th, tm = parts2(jnp.transpose(sums[:, :pad])[:qrows])
    smt[:qrows] = th
    smt[qrows:] = tm
    wh, wm = parts2(jnp.concatenate([win, jnp.zeros((R, features), F32)], axis=0))
    w2t[:2 * R] = wh
    w2t[2 * R:] = wm

    both = dot3(win, wout_t, nn)
    both = jnp.where(iota(both.shape, 1) // R % taps == taps // 2, both, 0.0)
    oh, om = parts2(wout_t)
    tblk = iota(wout_t.shape, 1) // R % taps
    sines = sinusoid(ts_ref, steps, features)
    copies[0].wait()
    v = jnp.zeros((features, 3 * tcols), F32)
    for start_tap in range(0, taps, taps_side):
        weights = wc[start_tap:start_tap + taps_side].reshape(taps_side * features, features)
        out = nn(weights, oh) + nn(weights, om)
        for i in range(taps_side):
            v = jnp.where(tblk == start_tap + i, out[i * features:(i + 1) * features], v)
    v_all = jnp.concatenate([v, both], axis=0)
    va, vb, _ = parts3(v_all)
    third = iota(v_all.shape, 1) // tcols
    v3[...] = jnp.where(third == 1, vb, va).astype(BF16)
    cols = -(-2 * tcols // LANES) * LANES
    vT = jnp.transpose(v[:, :cols] if cols <= 3 * tcols else jnp.concatenate([v, jnp.zeros((features, cols - 3 * tcols), F32)], axis=1))[:2 * tcols]
    va, vb, _ = parts3(vT)
    vt3[...] = jnp.where(iota(vT.shape, 0) // tcols == 1, vb, va).astype(BF16)

    copies[1].wait()
    hh, hm = parts2(sines)
    stacked = jnp.concatenate([hh.astype(F32), hm.astype(F32)], axis=0).astype(BF16)
    wh, wm = parts2(w1[...])
    first = nn(stacked, wh)
    hidden = first[:steps] + first[steps:] + nn(stacked, wm)[:steps]
    hidden = hidden * (0.5 * jnp.tanh(0.5 * hidden) + 0.5)
    copies[2].wait()
    hh, hm = parts2(hidden)
    stacked = jnp.concatenate([hh.astype(F32), hm.astype(F32)], axis=0).astype(BF16)
    wh, wm = parts2(w2[...])
    first = nt(wh, stacked)
    embed = first[:, :steps] + first[:, steps:] + nt(wm, stacked)[:, :steps]
    embed_out = dot3(woutT, embed, nn)
    for s in range(steps):
        ebs[s] = jnp.broadcast_to(embed_out[:, s:s + 1], (R, LANES))

    def unrolled(block, owner):
        if lanes > block.shape[1]:
            block = jnp.concatenate([block, jnp.zeros((2 * R, lanes - block.shape[1]), F32)], axis=1)
        return pltpu.roll(block, owner * span, 1)

    both = unrolled(mine[own], me)
    for d, copy in enumerate(spread):
        copy.wait()
        both = both + unrolled(slots[d], lax.rem(me + size - 1 - d, size))
    start, target = both[:R], both[R:]

    def forward(s, x):
        xa, xb, xc = parts3(x)
        x6 = jnp.concatenate([xa, xb, xa, xc, xb, xa], axis=0).astype(BF16)
        projected = nn(wext[...], x6)
        q = jnp.concatenate([x] + [x * x[c:c + 1] for c in range(chans)], axis=0)
        qs = jnp.broadcast_to(jnp.sum(q, axis=1, keepdims=True), (qrows, LANES))
        qa, qb, qc = parts3(qs)
        q6 = jnp.concatenate([qa, qb, qa, qc, qb, qa], axis=0).astype(BF16)
        stats = nn(sm6[...], q6)
        average = stats[:features]
        variance = stats[features:] - average * average
        rstd = lax.rsqrt(variance + 1e-05)
        scale = rstd * gain_col
        avg_s[s] = average
        rstd_s[s] = rstd
        scale_s[s] = scale
        z = (projected[:features] - wide(average, lanes)) * wide(scale, lanes)
        z_s[s] = z
        act = (z * (0.5 * jnp.tanh(0.5 * z) + 0.5)).astype(BF16)
        act_s[s] = act
        y = nn(vt3[...], act)
        y = y[:tcols] + y[tcols:]
        guess = projected[features:] + wide(ebs[s], lanes)
        for tap in range(taps):
            piece = y[tap * R:(tap + 1) * R]
            if offsets[tap] % lanes:
                piece = pltpu.roll(piece, (-offsets[tap]) % lanes, 1) * mask[tap * R:(tap + 1) * R]
            guess = guess + piece
        x = wide(keep_s[s], lanes) * x + wide(noise_s[s], lanes) * guess
        path[s + 1] = x
        return x

    path[0] = start
    last = lax.fori_loop(0, steps, forward, start)
    gacc[...] = jnp.zeros_like(gacc)

    def backward(i, adjoint):
        s = steps - 1 - i
        a = wide(noise_s[s], lanes) * adjoint
        shifted = []
        for tap in range(taps):
            piece = a
            if offsets[tap] % lanes:
                piece = pltpu.roll(a * mask[tap * R:(tap + 1) * R], offsets[tap] % lanes, 1)
            shifted.append(piece)
        shifted = jnp.concatenate(shifted, axis=0)
        high = shifted.astype(BF16).astype(F32)
        low = shifted - high
        a3 = jnp.concatenate([high, high, low], axis=0).astype(BF16)
        grads = nn(v3[...], a3)
        gacc[...] += nt(jnp.concatenate([high, low], axis=0).astype(BF16), act_s[s])
        z = z_s[s]
        sig = 0.5 * jnp.tanh(0.5 * z) + 0.5
        slope = sig + z * sig * (1.0 - sig)
        dz = grads[:features] * slope
        dzs = dz * wide(scale_s[s], lanes)
        rstd = rstd_s[s]
        e1 = jnp.broadcast_to(jnp.sum(dzs, axis=1, keepdims=True), (features, LANES))
        e2 = jnp.broadcast_to(jnp.sum(dz * z, axis=1, keepdims=True), (features, LANES)) * (rstd * rstd)
        pair = jnp.concatenate([e2 * avg_s[s] - e1, e2], axis=1)
        ph, pm = parts2(pair)
        k = nn(smt[...], ph)
        k = k[:qrows] + k[qrows:] + nn(smt[:qrows], pm)
        dh, dm = parts2(dzs)
        direct = nn(w2t[...], dh)
        direct = direct[:R] + direct[2 * R:3 * R] + nn(w2t[:2 * R], dm)[:R]
        result = wide(keep_s[s], lanes) * adjoint + grads[features:] + direct + wide(k[:R, :LANES], lanes)
        x = path[s]
        for c in range(chans):
            result = result - wide(k[(c + 1) * R:(c + 2) * R, LANES:], lanes) * x[c:c + 1]
        return result

    lax.fori_loop(0, steps, backward, last - target)
    garrived_total = gacc[:tcols] + gacc[tcols:]
    gsend[...] = garrived_total
    partners = [me - own + lax.rem(own + d, micro) for d in range(1, micro)]
    swaps = []
    for d, partner in enumerate(partners):
        for k, (src, dst) in enumerate(((path.at[section + 1], arrived.at[d]), (gsend, garrived.at[d]))):
            swaps.append(pltpu.make_async_remote_copy(
                src_ref=src, dst_ref=dst, send_sem=send2.at[d, k], recv_sem=recv2.at[d, k],
                device_id={"tensor": partner}, device_id_type=MESH))
    for copy in swaps:
        copy.start()
    paths_ref[own] = path[section + 1]
    for copy in swaps:
        copy.wait()
    total = garrived_total
    for d in range(micro - 1):
        total = total + garrived[d]
        paths_ref[lax.rem(own + micro - 1 - d, micro)] = arrived[d]
    g_ref[...] = total


def finish_kernel(dims, paths_ref, g_ref, wout_ref, traj_ref, grad_hbm, grads, sems):
    size, taps, span = dims
    me = lax.axis_index("tensor")
    _, micro, chans, rows, width = traj_ref.shape
    share = grads.shape[1]
    features = g_ref.shape[1]
    padded = -(-features // LANES) * LANES
    weights = jnp.concatenate([wout_ref[...], jnp.zeros((chans, padded - features), F32)], axis=1)
    weights = pltpu.roll(weights, lax.rem(padded - me * share, padded), 1)[:, :share]
    weights = jnp.concatenate([weights, jnp.zeros((R - chans, share), F32)], axis=0) if chans < R else weights
    wa, wb, _ = parts3(weights)
    left = jnp.concatenate([wa, wb, wa, wb], axis=0).astype(BF16)
    copies = []
    for tap in range(taps):
        ga, gb, _ = parts3(g_ref[tap * R:(tap + 1) * R])
        grads[tap] = tn(left, jnp.concatenate([ga, ga, gb, gb], axis=0).astype(BF16))
        copies.append(pltpu.make_async_copy(grads.at[tap], grad_hbm.at[tap], sems.at[tap]))
        copies[-1].start()
    for m in range(micro):
        cells = paths_ref[m]
        cells = pltpu.roll(cells, lax.rem(size - me, size) * span, 1)
        for r in range(rows):
            traj_ref[0, m, :, r, :] = cells[:chans, r * width:(r + 1) * width]
    for copy in copies:
        copy.wait()


def local(noise, target, timesteps, w_in, gn_gain, w_time1, w_time2, w_conv, w_out):
    size = lax.axis_size("tensor")
    micro, chans, rows, width = noise.shape
    features = w_in.shape[1]
    temb = w_time1.shape[1]
    taps = w_conv.shape[0]
    side = math.isqrt(taps)
    steps = timesteps.shape[0]
    height = rows * size
    lanes = height * width
    span = rows * width
    qrows = (1 + chans) * R
    tcols = taps * R
    block = -(-span // LANES) * LANES
    share = features // size
    vmem = pl.BlockSpec(memory_space=pltpu.VMEM)
    smem = pl.BlockSpec(memory_space=pltpu.SMEM)
    hbm = pl.BlockSpec(memory_space=pl.ANY)
    dma = pltpu.SemaphoreType.DMA
    wout_t = w_out.T
    paths, g = pl.pallas_call(
        functools.partial(chain_kernel, (height, width, features, steps, chans, side, size, micro)),
        out_shape=(jax.ShapeDtypeStruct((micro, R, lanes), F32), jax.ShapeDtypeStruct((tcols, features), F32)),
        in_specs=[smem, vmem, vmem, vmem, vmem, vmem, hbm, hbm, hbm],
        out_specs=(vmem, vmem),
        scratch_shapes=[
            pltpu.VMEM((features, temb), F32),
            pltpu.VMEM((features, temb), F32),
            pltpu.VMEM((taps, features, features), BF16),
            dma((3,)),
            pltpu.VMEM((micro, 2 * R, block), F32),
            pltpu.VMEM((size - 1, 2 * R, block), F32),
            dma((size - 1,)),
            dma((size - 1,)),
            pltpu.VMEM((steps + 1, R, lanes), F32),
            pltpu.VMEM((micro - 1, R, lanes), F32),
            pltpu.VMEM((tcols, features), F32),
            pltpu.VMEM((micro - 1, tcols, features), F32),
            dma((micro - 1, 2)),
            dma((micro - 1, 2)),
            pltpu.VMEM((steps, features, lanes), BF16),
            pltpu.VMEM((steps, features, lanes), F32),
            pltpu.VMEM((steps, features, LANES), F32),
            pltpu.VMEM((steps, features, LANES), F32),
            pltpu.VMEM((steps, features, LANES), F32),
            pltpu.VMEM((features + R, 6 * R), BF16),
            pltpu.VMEM((2 * features, 6 * qrows), BF16),
            pltpu.VMEM((2 * qrows, features), BF16),
            pltpu.VMEM((features + R, 3 * tcols), BF16),
            pltpu.VMEM((2 * tcols, features), BF16),
            pltpu.VMEM((4 * R, features), BF16),
            pltpu.VMEM((tcols, lanes), F32),
            pltpu.VMEM((steps, R, LANES), F32),
            pltpu.VMEM((2 * tcols, features), F32),
            pltpu.VMEM((steps, R, LANES), F32),
            pltpu.VMEM((steps, R, LANES), F32),
        ],
        compiler_params=pltpu.CompilerParams(vmem_limit_bytes=60 * 1024 * 1024, collective_id=0, has_side_effects=True),
        name="chain",
    )(timesteps, noise, target, w_in, gn_gain, wout_t, w_time1, w_time2.T, w_conv)
    trajectory, grad = pl.pallas_call(
        functools.partial(finish_kernel, (size, taps, span)),
        out_shape=(jax.ShapeDtypeStruct((1,) + noise.shape, F32), jax.ShapeDtypeStruct((taps, share, features), F32)),
        in_specs=[vmem, vmem, vmem],
        out_specs=(vmem, hbm),
        scratch_shapes=[pltpu.VMEM((taps, share, features), F32), dma((taps,))],
        name="finish",
    )(paths, g, wout_t)
    return trajectory, jnp.transpose(grad, (0, 2, 1))


def solution(mesh):
    placed = (P(None, None, "tensor", None), P(None, None, "tensor", None)) + (P(),) * 7
    return jax.shard_map(
        local,
        mesh=mesh,
        in_specs=placed,
        out_specs=(P("section", None, None, "tensor", None), P(None, None, "tensor")),
        check_vma=False,
    )
```

time: 47.6 us -> 25 us (0.53)
  local copies, waits for them, and re-layouts: 7.63 us -> 0 us
  Pallas kernels: 31.8 us -> 24.2 us
  other arithmetic: 4.96 us -> 0 us
  matrix products: 2.12 us -> 0 us
    pallas_call x3 -> x2, Pallas kernels: 31.8 us -> 24.2 us  [the longest x1 21.4 us: local(): pl.pallas_call(functools.partial(chain_kernel, (height, width, features,...]
    unnamed x7 -> x0, local copies, waits for them, and re-layouts: 3.66 us -> none
    dot_general x1 -> x0, matrix products: 2.12 us -> none  [local(): grad = jnp.einsum('kcd,ec->kde', total, w_share, precision=HIGH)]
    reduce_sum x2 -> x0, other arithmetic: 1.81 us -> none  [the longest x1 0.96 us: local(): total = jnp.sum(gs, axis=0).reshape(taps, R, features)[:, :chans]]
    another operation x5 -> x0, local copies, waits for them, and re-layouts: 1.79 us -> none  [the longest x2 1.56 us: local(): jnp.stack([noise.reshape(micro, chans, span), target.reshape(micro, chans...]
    reshape x3 -> x0, local copies, waits for them, and re-layouts: 1.25 us -> none  [the longest x1 0.68 us: local(): lax.dynamic_slice(paths, (0, 0, me * span), (micro, chans, span))]
    dynamic_slice x1 -> x0, local copies, waits for them, and re-layouts: 0.77 us -> none  [local(): lax.dynamic_slice(paths, (0, 0, me * span), (micro, chans, span))]
    sub x2 -> x0, other arithmetic: 0.68 us -> none  [the longest x1 0.67 us: step_terms(): noise = jnp.sqrt(1.0 - after) - keep * jnp.sqrt(1.0 - now)]
where the time goes in v2:
time: 25 us; the launch traced here: 24.8 us
  Pallas kernels  24.2 us (97%)
  between operations  0.64 us (3%)
    pallas_call x1, Pallas kernels, local(): pl.pallas_call(functools.partial(chain_kernel, (height, width, features,...  21.4 us
    pallas_call x1, Pallas kernels, local(): pl.pallas_call(functools.partial(finish_kernel, (size, taps, span)), out_...  2.83 us

profile of v2, /device:TPU:0, one launch (start us, length us, event | category | flops | bytes accessed | tf_op | source)
XLA Modules:
  0.0 24.8 jit_solution(16003822657388814976)
XLA Ops:
  0.6 21.4 %chain.1 = (f32[2,8,256]{2,1,0:T(8,128)}, f32[72,320]{1,0:T(8,128)}) custom-call(s32[8]{0:T(128)} %ts_ref.1, f32[2,4,2,32]{3,2,1,0:T(2,128)} %noise_ref.1, f32[2,4,2,32]{3,2,1,0:T(2,128)} %target_ref.1, f32[4,320]{1,0:T(4,128)} %win_ref.1, f32[320]{0:T(512)} %gain_ref.1, f32[4,320]{1,0:T(4,128)} %bitcast.4, f32[320,1280]{1,0:T(8,128)} %w1_hbm.1, ...), custom_call_target="tpu_custom_call" | custom-call | tf_op jit(solution)/shard_map/chain/pallas_call | solution.py:371
  22.0 2.8 %finish.1 = (f32[1,2,4,2,32]{4,3,2,1,0:T(2,128)}, f32[9,80,320]{2,1,0:T(8,128)}) custom-call(f32[2,8,256]{2,1,0:T(8,128)} %get-tuple-element.6.paths_ref, f32[72,320]{1,0:T(8,128)} %get-tuple-element.7.g_ref, f32[4,320]{1,0:T(4,128)} %bitcast.5), custom_call_target="tpu_custom_call" | custom-call | tf_op jit(solution)/shard_map/finish/pallas_call | solution.py:411

commit v3 on v2

--- a/solution.py
+++ b/solution.py
@@ -15,6 +15,8 @@
 BF16 = jnp.bfloat16
 R = 8
 LANES = 128
+UNROLL_F = 8
+UNROLL_B = 8
 
 
 def parts3(x):
@@ -120,6 +122,37 @@
         for r in range(rows):
             mine[m, :chans, r * width:(r + 1) * width] = noise_ref[m, :, r, :]
             mine[m, R:R + chans, r * width:(r + 1) * width] = target_ref[m, :, r, :]
+    step_coefficients(ts_ref, steps, keep_s, noise_s)
+    sines = sinusoid(ts_ref, steps, features)
+
+    lane = iota((1, lanes), 1)
+    row, col = lane // width, lane % width
+    offsets = []
+    for tap in range(taps):
+        dy, dx = tap // taps_side - taps_side // 2, tap % taps_side - taps_side // 2
+        offsets.append(dy * width + dx)
+        ok = (row + dy >= 0) & (row + dy < height) & (col + dx >= 0) & (col + dx < width)
+        mask[tap * R:(tap + 1) * R] = jnp.broadcast_to(ok.astype(F32), (R, lanes))
+
+    win, woutT = win_ref[...], wout_ref[...]
+    if chans < R:
+        fill = jnp.zeros((R - chans, features), F32)
+        win, woutT = jnp.concatenate([win, fill], axis=0), jnp.concatenate([woutT, fill], axis=0)
+
+    def tiled(weights, cols):
+        high, mid, low = (part.astype(BF16) for part in parts3(weights))
+        picker = (iota((R, cols), 1) % R == iota((R, cols), 0)).astype(BF16)
+        return tn(high, picker) + tn(mid, picker) + tn(low, picker)
+
+    win_t = tiled(win, 6 * qrows)
+    wout_t = tiled(woutT, 3 * tcols)
+    gain_row = gain_ref[...].reshape(1, features)
+    gain_col = tn(gain_row, jnp.ones((1, LANES), F32), HIGH)
+
+    pa, pb, pc = parts3(jnp.concatenate([win_t[:, :6 * R], dot3(woutT, win_t[:, :6 * R], nn)], axis=0))
+    blk = iota((1, 6 * R), 1) // R
+    wext[...] = jnp.where((blk == 2) | (blk == 4), pb, jnp.where(blk == 5, pc, pa)).astype(BF16)
+
     pl.semaphore_wait(barrier, size - 1)
     spread = [pltpu.make_async_remote_copy(
         src_ref=mine.at[lax.rem(peer, micro)], dst_ref=slots.at[d], send_sem=send.at[d], recv_sem=recv.at[d],
@@ -127,42 +160,12 @@
     for copy in spread:
         copy.start()
 
-    step_coefficients(ts_ref, steps, keep_s, noise_s)
-
-    lane = iota((R, lanes), 1)
-    row, col = lane // width, lane % width
-    offsets = []
-    for tap in range(taps):
-        dy, dx = tap // taps_side - taps_side // 2, tap % taps_side - taps_side // 2
-        offsets.append(dy * width + dx)
-        ok = (row + dy >= 0) & (row + dy < height) & (col + dx >= 0) & (col + dx < width)
-        mask[tap * R:(tap + 1) * R] = ok.astype(F32)
-
-    win, woutT = win_ref[...], wout_ref[...]
-    if chans < R:
-        fill = jnp.zeros((R - chans, features), F32)
-        win, woutT = jnp.concatenate([win, fill], axis=0), jnp.concatenate([woutT, fill], axis=0)
-
-    def tiled(weights, cols):
-        high, mid, low = (part.astype(BF16) for part in parts3(weights))
-        picker = (iota((R, cols), 1) % R == iota((R, cols), 0)).astype(BF16)
-        return tn(high, picker) + tn(mid, picker) + tn(low, picker)
-
-    win_t = tiled(win, 6 * qrows)
-    wout_t = tiled(woutT, 3 * tcols)
-    gain_row = gain_ref[...].reshape(1, features)
-    gain_col = tn(gain_row, jnp.ones((1, LANES), F32), HIGH)
-
-    pa, pb, pc = parts3(jnp.concatenate([win_t[:, :6 * R], dot3(woutT, win_t[:, :6 * R], nn)], axis=0))
-    blk = iota(pa.shape, 1) // R
-    wext[...] = jnp.where((blk == 2) | (blk == 4), pb, jnp.where(blk == 5, pc, pa)).astype(BF16)
-
-    qlane = iota(win_t.shape, 1)
+    qlane = iota((1, 6 * qrows), 1)
     qblk = (qlane % qrows) // R
     factor = jnp.ones_like(win_t)
     for c in range(chans):
         factor = jnp.where(qblk == c + 1, win_t[:, c:c + 1], factor)
-    member = (iota((features, features), 0) // per_group == iota((features, features), 1) // per_group).astype(BF16)
+    member = (iota((features, 1), 0) // per_group == iota((1, features), 1) // per_group).astype(BF16)
     sa, sb = parts2(win_t * factor)
     sums = (nn(member, sa) + nn(member, sb)) * (1.0 / count)
     sa, sb, sc = parts3(sums)
@@ -178,11 +181,10 @@
     w2t[:2 * R] = wh
     w2t[2 * R:] = wm
 
+    tblk = iota((1, 3 * tcols), 1) // R % taps
     both = dot3(win, wout_t, nn)
-    both = jnp.where(iota(both.shape, 1) // R % taps == taps // 2, both, 0.0)
+    both = jnp.where(tblk == taps // 2, both, 0.0)
     oh, om = parts2(wout_t)
-    tblk = iota(wout_t.shape, 1) // R % taps
-    sines = sinusoid(ts_ref, steps, features)
     copies[0].wait()
     v = jnp.zeros((features, 3 * tcols), F32)
     for start_tap in range(0, taps, taps_side):
@@ -192,12 +194,12 @@
             v = jnp.where(tblk == start_tap + i, out[i * features:(i + 1) * features], v)
     v_all = jnp.concatenate([v, both], axis=0)
     va, vb, _ = parts3(v_all)
-    third = iota(v_all.shape, 1) // tcols
+    third = iota((1, 3 * tcols), 1) // tcols
     v3[...] = jnp.where(third == 1, vb, va).astype(BF16)
     cols = -(-2 * tcols // LANES) * LANES
     vT = jnp.transpose(v[:, :cols] if cols <= 3 * tcols else jnp.concatenate([v, jnp.zeros((features, cols - 3 * tcols), F32)], axis=1))[:2 * tcols]
     va, vb, _ = parts3(vT)
-    vt3[...] = jnp.where(iota(vT.shape, 0) // tcols == 1, vb, va).astype(BF16)
+    vt3[...] = jnp.where(iota((2 * tcols, 1), 0) >= tcols, vb, va).astype(BF16)
 
     copies[1].wait()
     hh, hm = parts2(sines)
@@ -260,7 +262,7 @@
         return x
 
     path[0] = start
-    last = lax.fori_loop(0, steps, forward, start)
+    last = lax.fori_loop(0, steps, forward, start, unroll=min(steps, UNROLL_F))
     gacc[...] = jnp.zeros_like(gacc)
 
     def backward(i, adjoint):
@@ -299,9 +301,14 @@
             result = result - wide(k[(c + 1) * R:(c + 2) * R, LANES:], lanes) * x[c:c + 1]
         return result
 
-    lax.fori_loop(0, steps, backward, last - target)
-    garrived_total = gacc[:tcols] + gacc[tcols:]
-    gsend[...] = garrived_total
+    lax.fori_loop(0, steps, backward, last - target, unroll=min(steps, UNROLL_B))
+    per = R // chans
+    for tile in range(gsend.shape[0] // R):
+        packed = jnp.zeros((R, features), F32)
+        for i, tap in enumerate(range(tile * per, min(taps, (tile + 1) * per))):
+            block = gacc[tap * R:(tap + 1) * R] + gacc[tcols + tap * R:tcols + (tap + 1) * R]
+            packed = packed + (pltpu.roll(block, i * chans, 0) if i else block)
+        gsend[tile * R:(tile + 1) * R] = packed
     partners = [me - own + lax.rem(own + d, micro) for d in range(1, micro)]
     swaps = []
     for d, partner in enumerate(partners):
@@ -314,7 +321,7 @@
     paths_ref[own] = path[section + 1]
     for copy in swaps:
         copy.wait()
-    total = garrived_total
+    total = gsend[...]
     for d in range(micro - 1):
         total = total + garrived[d]
         paths_ref[lax.rem(own + micro - 1 - d, micro)] = arrived[d]
@@ -331,12 +338,17 @@
     weights = jnp.concatenate([wout_ref[...], jnp.zeros((chans, padded - features), F32)], axis=1)
     weights = pltpu.roll(weights, lax.rem(padded - me * share, padded), 1)[:, :share]
     weights = jnp.concatenate([weights, jnp.zeros((R - chans, share), F32)], axis=0) if chans < R else weights
-    wa, wb, _ = parts3(weights)
-    left = jnp.concatenate([wa, wb, wa, wb], axis=0).astype(BF16)
+    per = R // chans
+    lefts = []
+    for i in range(per):
+        wa, wb, _ = parts3(pltpu.roll(weights, i * chans, 0) if i else weights)
+        lefts.append(jnp.concatenate([wa, wb, wa, wb], axis=0).astype(BF16))
     copies = []
     for tap in range(taps):
-        ga, gb, _ = parts3(g_ref[tap * R:(tap + 1) * R])
-        grads[tap] = tn(left, jnp.concatenate([ga, ga, gb, gb], axis=0).astype(BF16))
+        if tap % per == 0:
+            ga, gb, _ = parts3(g_ref[tap // per * R:(tap // per + 1) * R])
+            right = jnp.concatenate([ga, ga, gb, gb], axis=0).astype(BF16)
+        grads[tap] = tn(lefts[tap % per], right)
         copies.append(pltpu.make_async_copy(grads.at[tap], grad_hbm.at[tap], sems.at[tap]))
         copies[-1].start()
     for m in range(micro):
@@ -361,6 +373,7 @@
     span = rows * width
     qrows = (1 + chans) * R
     tcols = taps * R
+    grows = -(-taps // (R // chans)) * R
     block = -(-span // LANES) * LANES
     share = features // size
     vmem = pl.BlockSpec(memory_space=pltpu.VMEM)
@@ -370,7 +383,7 @@
     wout_t = w_out.T
     paths, g = pl.pallas_call(
         functools.partial(chain_kernel, (height, width, features, steps, chans, side, size, micro)),
-        out_shape=(jax.ShapeDtypeStruct((micro, R, lanes), F32), jax.ShapeDtypeStruct((tcols, features), F32)),
+        out_shape=(pltpu.VMEM((micro, R, lanes), F32), pltpu.VMEM((grows, features), F32)),
         in_specs=[smem, vmem, vmem, vmem, vmem, vmem, hbm, hbm, hbm],
         out_specs=(vmem, vmem),
         scratch_shapes=[
@@ -384,8 +397,8 @@
             dma((size - 1,)),
             pltpu.VMEM((steps + 1, R, lanes), F32),
             pltpu.VMEM((micro - 1, R, lanes), F32),
-            pltpu.VMEM((tcols, features), F32),
-            pltpu.VMEM((micro - 1, tcols, features), F32),
+            pltpu.VMEM((grows, features), F32),
+            pltpu.VMEM((micro - 1, grows, features), F32),
             dma((micro - 1, 2)),
             dma((micro - 1, 2)),
             pltpu.VMEM((steps, features, lanes), BF16),
@@ -408,6 +421,7 @@
         compiler_params=pltpu.CompilerParams(vmem_limit_bytes=60 * 1024 * 1024, collective_id=0, has_side_effects=True),
         name="chain",
     )(timesteps, noise, target, w_in, gn_gain, wout_t, w_time1, w_time2.T, w_conv)
+    paths, g = (pltpu.with_memory_space_constraint(held, pltpu.VMEM) for held in (paths, g))
     trajectory, grad = pl.pallas_call(
         functools.partial(finish_kernel, (size, taps, span)),
         out_shape=(jax.ShapeDtypeStruct((1,) + noise.shape, F32), jax.ShapeDtypeStruct((taps, share, features), F32)),

time: 25 us -> 23.1 us (0.924)
  Pallas kernels: 24.2 us -> 22.2 us
    pallas_call x1, Pallas kernels: 21.4 us -> 19.6 us  [local(): pl.pallas_call(functools.partial(chain_kernel, (height, width, features,...]
where the time goes in v3:
time: 23.1 us; the launch traced here: 22.8 us
  Pallas kernels  22.2 us (96%)
  between operations  0.64 us (3%)
    pallas_call x1, Pallas kernels, local(): pl.pallas_call(functools.partial(chain_kernel, (height, width, features,...  19.6 us
    pallas_call x1, Pallas kernels, local(): pl.pallas_call(functools.partial(finish_kernel, (size, taps, span)), out_...  2.62 us

profile of v3, /device:TPU:0, one launch (start us, length us, event | category | flops | bytes accessed | tf_op | source)
XLA Modules:
  0.0 22.8 jit_solution(16520192735246463596)
XLA Ops:
  0.6 19.6 %chain.1 = (f32[2,8,256]{2,1,0:T(8,128)S(1)}, f32[40,320]{1,0:T(8,128)S(1)}) custom-call(s32[8]{0:T(128)} %ts_ref.1, f32[2,4,2,32]{3,2,1,0:T(2,128)} %noise_ref.1, f32[2,4,2,32]{3,2,1,0:T(2,128)} %target_ref.1, f32[4,320]{1,0:T(4,128)} %win_ref.1, f32[320]{0:T(512)} %gain_ref.1, f32[4,320]{1,0:T(4,128)} %bitcast.4, f32[320,1280]{1,0:T(8,128)} %w1_hbm.1, ...), custom_call_target="tpu_custom_call" | custom-call | tf_op jit(solution)/shard_map/chain/pallas_call | solution.py:384
  20.2 2.6 %finish.1 = (f32[1,2,4,2,32]{4,3,2,1,0:T(2,128)}, f32[9,80,320]{2,1,0:T(8,128)}) custom-call(f32[2,8,256]{2,1,0:T(8,128)S(1)} %get-tuple-element.6.paths_ref, f32[40,320]{1,0:T(8,128)S(1)} %get-tuple-element.7.g_ref, f32[4,320]{1,0:T(4,128)} %bitcast.5), custom_call_target="tpu_custom_call" | custom-call | tf_op jit(solution)/shard_map/finish/pallas_call | solution.py:425

commit v4 on v3

--- a/solution.py
+++ b/solution.py
@@ -94,7 +94,7 @@
 
 
 def chain_kernel(dims, ts_ref, noise_ref, target_ref, win_ref, gain_ref, wout_ref, w1_hbm, w2_hbm, wc_hbm,
-                 paths_ref, g_ref, w1, w2, wc, sems, mine, slots, send, recv, path, arrived, gsend, garrived, send2, recv2,
+                 paths_ref, g_ref, wout_kept, w1, w2, wc, sems, mine, slots, send, recv, path, arrived, gsend, garrived, send2, recv2,
                  act_s, z_s, scale_s, avg_s, rstd_s, wext, sm6, smt, v3, vt3, w2t, mask, ebs, gacc, keep_s, noise_s):
     height, width, features, steps, chans, taps_side, size, micro = dims
     taps = taps_side * taps_side
@@ -144,6 +144,7 @@
         picker = (iota((R, cols), 1) % R == iota((R, cols), 0)).astype(BF16)
         return tn(high, picker) + tn(mid, picker) + tn(low, picker)
 
+    wout_kept[...] = woutT
     win_t = tiled(win, 6 * qrows)
     wout_t = tiled(woutT, 3 * tcols)
     gain_row = gain_ref[...].reshape(1, features)
@@ -184,12 +185,15 @@
     tblk = iota((1, 3 * tcols), 1) // R % taps
     both = dot3(win, wout_t, nn)
     both = jnp.where(tblk == taps // 2, both, 0.0)
-    oh, om = parts2(wout_t)
+    oh, om = parts2(wout_t[:, :LANES])
+    halves = jnp.where(iota((1, LANES), 1) // R % 2 == 0, oh.astype(F32), om.astype(F32)).astype(BF16)
     copies[0].wait()
     v = jnp.zeros((features, 3 * tcols), F32)
     for start_tap in range(0, taps, taps_side):
         weights = wc[start_tap:start_tap + taps_side].reshape(taps_side * features, features)
-        out = nn(weights, oh) + nn(weights, om)
+        out = nn(weights, halves)
+        out = out + pltpu.roll(out, R, 1)
+        out = jnp.concatenate([out] * (-(-3 * tcols // LANES)), axis=1)[:, :3 * tcols]
         for i in range(taps_side):
             v = jnp.where(tblk == start_tap + i, out[i * features:(i + 1) * features], v)
     v_all = jnp.concatenate([v, both], axis=0)
@@ -328,22 +332,27 @@
     g_ref[...] = total
 
 
-def finish_kernel(dims, paths_ref, g_ref, wout_ref, traj_ref, grad_hbm, grads, sems):
+def finish_kernel(dims, paths_ref, g_ref, wout_ref, traj_ref, grad_hbm, grads, traj, sems):
     size, taps, span = dims
     me = lax.axis_index("tensor")
     _, micro, chans, rows, width = traj_ref.shape
     share = grads.shape[1]
     features = g_ref.shape[1]
     padded = -(-features // LANES) * LANES
-    weights = jnp.concatenate([wout_ref[...], jnp.zeros((chans, padded - features), F32)], axis=1)
+    weights = jnp.concatenate([wout_ref[...], jnp.zeros((R, padded - features), F32)], axis=1)
     weights = pltpu.roll(weights, lax.rem(padded - me * share, padded), 1)[:, :share]
-    weights = jnp.concatenate([weights, jnp.zeros((R - chans, share), F32)], axis=0) if chans < R else weights
     per = R // chans
     lefts = []
     for i in range(per):
         wa, wb, _ = parts3(pltpu.roll(weights, i * chans, 0) if i else weights)
         lefts.append(jnp.concatenate([wa, wb, wa, wb], axis=0).astype(BF16))
-    copies = []
+    for m in range(micro):
+        cells = paths_ref[m]
+        cells = pltpu.roll(cells, lax.rem(size - me, size) * span, 1)
+        for r in range(rows):
+            traj[0, m, :, r, :] = cells[:chans, r * width:(r + 1) * width]
+    copies = [pltpu.make_async_copy(traj, traj_ref, sems.at[taps])]
+    copies[0].start()
     for tap in range(taps):
         if tap % per == 0:
             ga, gb, _ = parts3(g_ref[tap // per * R:(tap // per + 1) * R])
@@ -351,11 +360,6 @@
         grads[tap] = tn(lefts[tap % per], right)
         copies.append(pltpu.make_async_copy(grads.at[tap], grad_hbm.at[tap], sems.at[tap]))
         copies[-1].start()
-    for m in range(micro):
-        cells = paths_ref[m]
-        cells = pltpu.roll(cells, lax.rem(size - me, size) * span, 1)
-        for r in range(rows):
-            traj_ref[0, m, :, r, :] = cells[:chans, r * width:(r + 1) * width]
     for copy in copies:
         copy.wait()
 
@@ -381,11 +385,11 @@
     hbm = pl.BlockSpec(memory_space=pl.ANY)
     dma = pltpu.SemaphoreType.DMA
     wout_t = w_out.T
-    paths, g = pl.pallas_call(
+    held = pl.pallas_call(
         functools.partial(chain_kernel, (height, width, features, steps, chans, side, size, micro)),
-        out_shape=(pltpu.VMEM((micro, R, lanes), F32), pltpu.VMEM((grows, features), F32)),
+        out_shape=(pltpu.VMEM((micro, R, lanes), F32), pltpu.VMEM((grows, features), F32), pltpu.VMEM((R, features), F32)),
         in_specs=[smem, vmem, vmem, vmem, vmem, vmem, hbm, hbm, hbm],
-        out_specs=(vmem, vmem),
+        out_specs=(vmem, vmem, vmem),
         scratch_shapes=[
             pltpu.VMEM((features, temb), F32),
             pltpu.VMEM((features, temb), F32),
@@ -421,15 +425,15 @@
         compiler_params=pltpu.CompilerParams(vmem_limit_bytes=60 * 1024 * 1024, collective_id=0, has_side_effects=True),
         name="chain",
     )(timesteps, noise, target, w_in, gn_gain, wout_t, w_time1, w_time2.T, w_conv)
-    paths, g = (pltpu.with_memory_space_constraint(held, pltpu.VMEM) for held in (paths, g))
+    held = [pltpu.with_memory_space_constraint(one, pltpu.VMEM) for one in held]
     trajectory, grad = pl.pallas_call(
         functools.partial(finish_kernel, (size, taps, span)),
         out_shape=(jax.ShapeDtypeStruct((1,) + noise.shape, F32), jax.ShapeDtypeStruct((taps, share, features), F32)),
         in_specs=[vmem, vmem, vmem],
-        out_specs=(vmem, hbm),
-        scratch_shapes=[pltpu.VMEM((taps, share, features), F32), dma((taps,))],
+        out_specs=(hbm, hbm),
+        scratch_shapes=[pltpu.VMEM((taps, share, features), F32), pltpu.VMEM((1,) + noise.shape, F32), dma((taps + 1,))],
         name="finish",
-    )(paths, g, wout_t)
+    )(*held)
     return trajectory, jnp.transpose(grad, (0, 2, 1))
 
 

time: 23.1 us -> 20.3 us (0.88)
  Pallas kernels: 22.2 us -> 19.5 us
    pallas_call x1, Pallas kernels: 19.6 us -> 18.1 us  [local(): pl.pallas_call(functools.partial(chain_kernel, (height, width, features,...]
    pallas_call x1, Pallas kernels: 2.62 us -> 1.35 us  [local(): pl.pallas_call(functools.partial(finish_kernel, (size, taps, span)), out_...]
where the time goes in v4:
time: 20.3 us; the launch traced here: 20.1 us
  Pallas kernels  19.5 us (96%)
  between operations  0.64 us (3%)
    pallas_call x1, Pallas kernels, local(): pl.pallas_call(functools.partial(chain_kernel, (height, width, features,...  18.1 us
    pallas_call x1, Pallas kernels, local(): pl.pallas_call(functools.partial(finish_kernel, (size, taps, span)), out_...  1.35 us

profile of v4, /device:TPU:0, one launch (start us, length us, event | category | flops | bytes accessed | tf_op | source)
XLA Modules:
  0.0 20.1 jit_solution(13426644035249460640)
XLA Ops:
  0.6 18.1 %chain.1 = (f32[2,8,256]{2,1,0:T(8,128)S(1)}, f32[40,320]{1,0:T(8,128)S(1)}, f32[8,320]{1,0:T(8,128)S(1)}) custom-call(s32[8]{0:T(128)} %ts_ref.1, f32[2,4,2,32]{3,2,1,0:T(2,128)} %noise_ref.1, f32[2,4,2,32]{3,2,1,0:T(2,128)} %target_ref.1, f32[4,320]{1,0:T(4,128)} %win_ref.1, f32[320]{0:T(512)} %gain_ref.1, f32[4,320]{1,0:T(4,128)} %bitcast.4, ...), custom_call_target="tpu_custom_call" | custom-call | tf_op jit(solution)/shard_map/chain/pallas_call | solution.py:388
  18.8 1.4 %finish.1 = (f32[1,2,4,2,32]{4,3,2,1,0:T(2,128)}, f32[9,80,320]{2,1,0:T(8,128)}) custom-call(f32[2,8,256]{2,1,0:T(8,128)S(1)} %get-tuple-element.7.paths_ref, f32[40,320]{1,0:T(8,128)S(1)} %get-tuple-element.8.g_ref, f32[8,320]{1,0:T(8,128)S(1)} %get-tuple-element.9.wout_ref), custom_call_target="tpu_custom_call" | custom-call | tf_op jit(solution)/shard_map/finish/pallas_call | solution.py:429
